TPU v7x, 512 devices: a whole 4x8x8 slice. The times are simulated.
512 devices in a mesh: dp: 32 (over x, z), hidden: 16 (over y, core).
Axes of the slice: x: 4, y: 8, z: 8, core: 2. Of those that a mesh axis runs over, the one named last changes fastest.
Arguments:
- activations: bfloat16 [4096, 768], P(('dp', 'hidden')), may hold values from -6 to 6
- grad_out: bfloat16 [4096, 53248], P('dp', 'hidden'), may hold values from -8 to 8
- momentum: float32 [768, 53248], P('dp', 'hidden'), may hold values from -6 to 6
Outputs:
- new_momentum: float32 [768, 53248], P('dp', 'hidden')
All inputs are finite; a program needn't handle non-finite values.
Results may differ from a plain program's by a relative error of at most 0.0003.
Values may be sent and summed in bfloat16 or wider, within the bound.
No kernel may reach another device: no remote copies, remote signals or barrier semaphores. Data moves between devices by JAX's collectives and lax.ppermute only.
A program may use at most 64 MiB of HBM per device.

v0:
```python
import jax
import jax.numpy as jnp
from jax import lax
from jax.experimental import pallas as pl
from jax.experimental.pallas import tpu as pltpu
from jax.sharding import Mesh, PartitionSpec as P


EPSILON = 1e-06
DECAY = 0.9
NR = 32
TOK = 128
LANES = 128
XZ = ("x", "z")
CORES = [(0, 1), (1, 0)]
PIECES = ((0, 56), (56, 56), (112, 56), (168, 40))


def gram_kernel(cols_ref, *refs):
    act_refs, (g_out_ref, gram_ref, g_ref, q_ref, sem) = refs[:-5], refs[-5:]
    groups = cols_ref.shape[1] // 8
    depth = act_refs[0].shape[-1]
    lane_blocks = depth // LANES
    unroll = 26
    assert groups % unroll == 0

    opposite = len(act_refs) // 2
    for r in range(NR):
        half = r // (NR // 2)
        parts = act_refs[:opposite] + act_refs[opposite + half : opposite + half + 1]
        rows = [ref[r % ref.shape[0]] for ref in parts + act_refs[opposite + 2 :]]
        act = jnp.concatenate(rows, axis=0)
        g_ref[r] = jnp.dot(cols_ref[r], act, preferred_element_type=jnp.float32)

    save = pltpu.make_async_copy(g_ref, g_out_ref, sem)
    save.start()
    q_ref[...] = jnp.zeros_like(q_ref)

    def pair_block(rb, sb, same):
        pairs = [(i, j) for i in range(4) for j in range(4) if not same or i <= j]

        def body(f, acc):
            acc = list(acc)
            for h in range(unroll):
                row = pl.multiple_of((f * unroll + h) * 8, 8)
                for lb in range(lane_blocks):
                    lanes = slice(lb * LANES, (lb + 1) * LANES)
                    left = [g_ref[rb * 4 + i, pl.ds(row, 8), lanes] for i in range(4)]
                    right = left
                    if not same:
                        right = [g_ref[sb * 4 + i, pl.ds(row, 8), lanes] for i in range(4)]
                    for n, (i, j) in enumerate(pairs):
                        acc[n] = acc[n] + left[i] * right[j]
            return tuple(acc)

        zero = jnp.zeros((8, LANES), jnp.float32)
        acc = lax.fori_loop(0, groups // unroll, body, (zero,) * len(pairs))
        for n, (i, j) in enumerate(pairs):
            left_id = rb * 4 + i
            base = lax.rem(left_id, 8) * 128 + lax.div(left_id, 8) * 32
            q_ref[pl.ds(base + sb * 4 + j, 1), :] = jnp.sum(acc[n], axis=0, keepdims=True)

    def outer(rb, carry):
        pair_block(rb, rb, True)

        def inner(sb, c):
            pair_block(rb, sb, False)
            return c

        return lax.fori_loop(rb + 1, NR // 4, inner, carry)

    lax.fori_loop(0, NR // 4, outer, 0)
    sums = lax.dot_general(
        jnp.ones((8, LANES), jnp.float32),
        q_ref[...],
        (((1,), (1,)), ((), ())),
        precision=lax.Precision.HIGHEST,
        preferred_element_type=jnp.float32,
    )
    for i in range(8):
        row = sums[i : i + 1, i * LANES : (i + 1) * LANES]
        for k in range(gram_ref.shape[0]):
            gram_ref[k, i : i + 1, :] = row
    save.wait()


def tree_weights(packed):
    gram = jnp.concatenate([packed[:, 32 * q : 32 * q + 32] for q in range(4)], axis=0)
    rows = lax.broadcasted_iota(jnp.int32, (NR, NR), 0)
    cols = lax.broadcasted_iota(jnp.int32, (NR, NR), 1)
    upper = jnp.where(rows < cols, gram, 0.0)
    quad = jnp.where(rows == cols, gram, 2.0 * upper)
    w_col = jnp.ones((NR, 1), jnp.float32)
    w_row = jnp.ones((1, NR), jnp.float32)
    for level in range(5):
        scale = w_col * w_row
        same_half = (rows >> level) == (cols >> level)
        same_pair = (rows >> (level + 1)) == (cols >> (level + 1))
        squares = jnp.where(same_half, quad * scale, 0.0)
        crosses = jnp.where(same_pair & (~same_half), upper * scale, 0.0)

        def both(values, mask):
            down = jnp.sum(values, axis=1, keepdims=True)
            across = jnp.sum(values, axis=0, keepdims=True)
            as_row = jnp.sum(jnp.where(mask, down, 0.0), axis=0, keepdims=True)
            as_col = jnp.sum(jnp.where(mask, across, 0.0), axis=1, keepdims=True)
            return as_col, as_row

        sq_col, sq_row = both(squares, same_half)
        cr_col, cr_row = both(crosses, same_pair)
        w_col = w_col * (1.0 - cr_col / (2.0 * (sq_col + EPSILON)))
        w_row = w_row * (1.0 - cr_row / (2.0 * (sq_row + EPSILON)))
    return w_col


def combine_kernel(part_ref, kept_ref, mine_ref, theirs_ref, w_ref, ct_ref, g_ref, sem):
    share = kept_ref.shape[1] // 2
    lane_blocks = kept_ref.shape[2] // LANES
    loads = []
    for k, (start, size) in enumerate(PIECES):
        rows = pl.ds(start, size)
        loads.append(pltpu.make_async_copy(kept_ref.at[:, rows], g_ref.at[:, rows], sem.at[k]))
        loads[-1].start()
    weights = tree_weights(jnp.sum(part_ref[...], axis=0))
    for r in range(NR):
        w_ref[r] = jnp.broadcast_to(weights[r : r + 1, :], (8, LANES))
    ct_ref[pl.ds(2 * share, 48), :] = jnp.zeros((48, ct_ref.shape[1]), jnp.float32)

    def body(f, carry):
        row = pl.multiple_of(f * 8, 8)
        acc = [None] * lane_blocks
        for r in range(NR):
            weight = w_ref[r]
            for k in range(lane_blocks):
                term = g_ref[r, pl.ds(row, 8), k * LANES : (k + 1) * LANES] * weight
                acc[k] = term if r == 0 else acc[k] + term
        for k in range(lane_blocks):
            ct_ref[pl.ds(row, 8), k * LANES : (k + 1) * LANES] = acc[k]
        return carry

    for load, (start, size) in zip(loads, PIECES):
        load.wait()
        lax.fori_loop(start // 8, (start + size) // 8, body, 0)
    for part, ref in enumerate((mine_ref, theirs_ref)):
        for k in range(lane_blocks):
            lanes = slice(k * LANES, (k + 1) * LANES)
            ref[lanes, :] = ct_ref[share * part : share * part + LANES, lanes].T


def finish_kernel(pieces_ref, momentum_ref, out_ref):
    width = momentum_ref.shape[1] // pieces_ref.shape[0]
    row = jnp.concatenate([pieces_ref[k][:, :width] for k in range(pieces_ref.shape[0])], axis=1)
    out_ref[...] = DECAY * momentum_ref[...] + row


def ring(block):
    size = lax.axis_size("y")
    half = block.shape[0] // 2
    up = [(i, (i + 1) % size) for i in range(size)]
    down = [(i, (i - 1) % size) for i in range(size)]
    above, below = [block], [block]
    for step in range(size // 2):
        last = step == size // 2 - 1
        from_below, from_above = below[-1], above[-1]
        if last:
            from_below, from_above = from_below[:half], from_above[half:]
        below.append(lax.ppermute(from_below, "y", up))
        above.append(lax.ppermute(from_above, "y", down))
    return above[:-1] + [below[-1], above[-1]] + below[-2:0:-1]


def local(activations, grad_out, momentum):
    core = lax.axis_index("core")
    columns = grad_out.shape[1]
    share = columns // NR
    depth = activations.shape[1] // 2

    halves = activations.reshape(8, 2, depth).transpose(1, 0, 2)
    halves = jnp.broadcast_to(halves[None], (NR, 2, 8, depth)).reshape(2 * NR, 8, depth)
    halves = lax.all_to_all(halves, ("x", "z", "core"), 0, 0, tiled=True)
    halves = halves.reshape(NR * 16, depth)

    shift = 16 * lax.axis_index("y")
    rolled = lax.dynamic_slice_in_dim(jnp.concatenate([grad_out, grad_out], axis=0), shift, TOK, 0)
    acts = ring(halves.reshape(NR, 16, depth))
    own = lax.all_to_all(rolled.T.reshape(NR, share, TOK), XZ, 0, 0, tiled=True)
    other = lax.ppermute(own, "core", CORES)
    cols = jnp.concatenate([own, other], axis=1)

    grads, gram = pl.pallas_call(
        gram_kernel,
        out_shape=[
            jax.ShapeDtypeStruct((NR, 2 * share, depth), jnp.float32),
            jax.ShapeDtypeStruct((16, 8, LANES), jnp.float32),
        ],
        out_specs=[
            pl.BlockSpec(memory_space=pltpu.HBM),
            pl.BlockSpec(memory_space=pltpu.VMEM),
        ],
        scratch_shapes=[
            pltpu.VMEM((NR, 2 * share, depth), jnp.float32),
            pltpu.VMEM((1024, LANES), jnp.float32),
            pltpu.SemaphoreType.DMA,
        ],
        compiler_params=pltpu.CompilerParams(vmem_limit_bytes=48 << 20),
        name="gram",
    )(cols, *acts)

    gram = lax.all_to_all(gram, ("z", "core"), 0, 0, tiled=True)
    gram = jnp.sum(gram, axis=0)
    gram = lax.all_to_all(jnp.broadcast_to(gram, (32, 8, LANES)), ("x", "y"), 0, 0, tiled=True)

    mine, theirs = pl.pallas_call(
        combine_kernel,
        out_shape=[jax.ShapeDtypeStruct((depth, LANES), jnp.float32)] * 2,
        scratch_shapes=[
            pltpu.VMEM((NR, 8, LANES), jnp.float32),
            pltpu.VMEM((256, depth), jnp.float32),
            pltpu.VMEM(grads.shape, jnp.float32),
            pltpu.SemaphoreType.DMA((len(PIECES),)),
        ],
        in_specs=[
            pl.BlockSpec(memory_space=pltpu.VMEM),
            pl.BlockSpec(memory_space=pltpu.HBM),
        ],
        compiler_params=pltpu.CompilerParams(vmem_limit_bytes=56 << 20),
        name="combine",
    )(gram, grads)
    came = lax.ppermute(theirs, "core", CORES)
    low = jnp.where(core == 0, mine, came)
    high = jnp.where(core == 0, came, mine)
    pieces = jnp.concatenate([low, high], axis=0).reshape(NR, 24, LANES)
    pieces = lax.all_to_all(pieces, XZ, 0, 0, tiled=True)

    return pl.pallas_call(
        finish_kernel,
        out_shape=jax.ShapeDtypeStruct(momentum.shape, jnp.float32),
        compiler_params=pltpu.CompilerParams(vmem_limit_bytes=4 << 20),
        name="finish",
    )(pieces, momentum)


def solution(mesh):
    devices = mesh.devices.reshape(4, 8, 8, 2)
    fine = Mesh(devices, ("x", "z", "y", "core"))
    dp, hidden = ("x", "z"), ("y", "core")

    return jax.shard_map(
        local,
        mesh=fine,
        in_specs=(P(dp + hidden, None), P(dp, hidden), P(dp, hidden)),
        out_specs=P(dp, hidden),
        check_vma=False,
    )
```

profile of v0, /device:TPU:1, one launch (start us, length us, event | category | flops | bytes accessed | tf_op | source)
XLA Modules:
  0.0 174.0 jit_solution(17490791874051426308)
XLA Ops:
  0.0 1.6 broadcast_in_dim.4
  1.6 14.8 %all-to-all-start.1 = ((bf16[64,8,384]{2,1,0:T(8,128)(2,1)}), bf16[64,8,384]{2,1,0:T(8,128)(2,1)S(1)}, u32[]{:S(2)}, u32[]{:S(2)}) async-start(bf16[64,8,384]{2,1,0:T(8,128)(2,1)} %bitcast.4), calls=%async_computation.1 | async-start | bytes 786432 | tf_op jit(solution)/shard_map/all_to_all | solution.py:180
  16.9 1.3 copy.4
  18.1 12.8 %all-to-all-done.1 = bf16[64,8,384]{2,1,0:T(8,128)(2,1)S(1)} async-done(((bf16[64,8,384]{2,1,0:T(8,128)(2,1)}), bf16[64,8,384]{2,1,0:T(8,128)(2,1)S(1)}, u32[]{:S(2)}, u32[]{:S(2)}) %all-to-all-start.1) | async-done | bytes 393248 | tf_op jit(solution)/shard_map/all_to_all | solution.py:180
  31.0 5.2 %all-to-all-start = ((bf16[32,104,128]{2,1,0:T(8,128)(2,1)}), bf16[32,104,128]{2,1,0:T(8,128)(2,1)S(1)}, u32[]{:S(2)}, u32[]{:S(2)}) async-start(bf16[32,104,128]{2,1,0:T(8,128)(2,1)} %bitcast.1), calls=%async_computation | async-start | bytes 1703936 | tf_op jit(solution)/shard_map/all_to_all | solution.py:186
  36.2 3.2 %collective-permute-start.4 = (bf16[32,16,384]{2,1,0:T(8,128)(2,1)S(1)}, bf16[32,16,384]{2,1,0:T(8,128)(2,1)S(1)}, u32[]{:S(2)}, u32[]{:S(2)}) collective-permute-start(bf16[32,16,384]{2,1,0:T(8,128)(2,1)S(1)} %bitcast.9), channel_id=1, source_target_pairs={{0,2},{2,4},{4,6},{6,8},{8,10},{10,12},{12,14},{14,0},{1,3},{3,5},... | collective-permute-start | bytes 1179656 | tf_op jit(solution)/shard_map/ppermute | solution.py:167
  39.4 3.8 %collective-permute-start.1 = (bf16[32,16,384]{2,1,0:T(8,128)(2,1)S(1)}, bf16[32,16,384]{2,1,0:T(8,128)(2,1)S(1)}, u32[]{:S(2)}, u32[]{:S(2)}) collective-permute-start(bf16[32,16,384]{2,1,0:T(8,128)(2,1)S(1)} %bitcast.10), channel_id=1, source_target_pairs={{0,14},{2,0},{4,2},{6,4},{8,6},{10,8},{12,10},{14,12},{1,15},{3,1}... | collective-permute-start | bytes 1179656 | tf_op jit(solution)/shard_map/ppermute | solution.py:168
  43.2 13.9 %all-to-all-done = bf16[32,104,128]{2,1,0:T(8,128)(2,1)S(1)} async-done(((bf16[32,104,128]{2,1,0:T(8,128)(2,1)}), bf16[32,104,128]{2,1,0:T(8,128)(2,1)S(1)}, u32[]{:S(2)}, u32[]{:S(2)}) %all-to-all-start) | async-done | bytes 852000 | tf_op jit(solution)/shard_map/all_to_all | solution.py:186
  57.1 6.6 %collective-permute-start = (bf16[32,104,128]{2,1,0:T(8,128)(2,1)S(1)}, bf16[32,104,128]{2,1,0:T(8,128)(2,1)S(1)}, u32[]{:S(2)}, u32[]{:S(2)}) collective-permute-start(bf16[32,104,128]{2,1,0:T(8,128)(2,1)S(1)} %all-to-all-done), channel_id=1, source_target_pairs={{0,1},{1,0},{2,3},{3,2},{4,5},{5,4},{6,7},{7,6},{8,9},{9,8},{10,11... | collective-permute-start | bytes 2555912 | tf_op jit(solution)/shard_map/ppermute | solution.py:187
  63.7 3.2 %collective-permute-start.5 = (bf16[32,16,384]{2,1,0:T(8,128)(2,1)S(1)}, bf16[32,16,384]{2,1,0:T(8,128)(2,1)S(1)}, u32[]{:S(2)}, u32[]{:S(2)}) collective-permute-start(bf16[32,16,384]{2,1,0:T(8,128)(2,1)S(1)} %collective-permute-done.4.refs_8_), channel_id=1, source_target_pairs={{0,2},{2,4},{4,6},{6,8},{8,10},{10,12},{12,14},{14,0},{1,3},{3,5},... | collective-permute-start | bytes 1179656 | tf_op jit(solution)/shard_map/ppermute | solution.py:167
  67.0 3.8 %collective-permute-start.2 = (bf16[32,16,384]{2,1,0:T(8,128)(2,1)S(1)}, bf16[32,16,384]{2,1,0:T(8,128)(2,1)S(1)}, u32[]{:S(2)}, u32[]{:S(2)}) collective-permute-start(bf16[32,16,384]{2,1,0:T(8,128)(2,1)S(1)} %collective-permute-done.1.refs_1_), channel_id=1, source_target_pairs={{0,14},{2,0},{4,2},{6,4},{8,6},{10,8},{12,10},{14,12},{1,15},{3,1}... | collective-permute-start | bytes 1179656 | tf_op jit(solution)/shard_map/ppermute | solution.py:168
  70.8 7.5 %collective-permute-done.5.refs_7_ = bf16[32,16,384]{2,1,0:T(8,128)(2,1)S(1)} collective-permute-done((bf16[32,16,384]{2,1,0:T(8,128)(2,1)S(1)}, bf16[32,16,384]{2,1,0:T(8,128)(2,1)S(1)}, u32[]{:S(2)}, u32[]{:S(2)}) %collective-permute-start.5) | collective-permute-done | bytes 393248 | tf_op jit(solution)/shard_map/ppermute | solution.py:167
  78.3 1.9 %collective-permute-start.6 = (bf16[32,16,384]{2,1,0:T(8,128)(2,1)S(1)}, bf16[32,16,384]{2,1,0:T(8,128)(2,1)S(1)}, u32[]{:S(2)}, u32[]{:S(2)}) collective-permute-start(bf16[32,16,384]{2,1,0:T(8,128)(2,1)S(1)} %collective-permute-done.5.refs_7_), channel_id=1, source_target_pairs={{0,2},{2,4},{4,6},{6,8},{8,10},{10,12},{12,14},{14,0},{1,3},{3,5},... | collective-permute-start | bytes 1179656 | tf_op jit(solution)/shard_map/ppermute | solution.py:167
  80.2 4.6 %collective-permute-start.3 = (bf16[32,16,384]{2,1,0:T(8,128)(2,1)S(1)}, bf16[32,16,384]{2,1,0:T(8,128)(2,1)S(1)}, u32[]{:S(2)}, u32[]{:S(2)}) collective-permute-start(bf16[32,16,384]{2,1,0:T(8,128)(2,1)S(1)} %collective-permute-done.2.refs_2_), channel_id=1, source_target_pairs={{0,14},{2,0},{4,2},{6,4},{8,6},{10,8},{12,10},{14,12},{1,15},{3,1}... | collective-permute-start | bytes 1179656 | tf_op jit(solution)/shard_map/ppermute | solution.py:168
  84.8 6.7 %collective-permute-done.6.refs_6_ = bf16[32,16,384]{2,1,0:T(8,128)(2,1)S(1)} collective-permute-done((bf16[32,16,384]{2,1,0:T(8,128)(2,1)S(1)}, bf16[32,16,384]{2,1,0:T(8,128)(2,1)S(1)}, u32[]{:S(2)}, u32[]{:S(2)}) %collective-permute-start.6) | collective-permute-done | bytes 393248 | tf_op jit(solution)/shard_map/ppermute | solution.py:167
  91.5 1.9 %collective-permute-start.7 = (bf16[16,16,384]{2,1,0:T(8,128)(2,1)S(1)}, bf16[16,16,384]{2,1,0:T(8,128)(2,1)S(1)}, u32[]{:S(2)}, u32[]{:S(2)}) collective-permute-start(bf16[16,16,384]{2,1,0:T(8,128)(2,1)S(1)} %slice.8), channel_id=1, source_target_pairs={{0,2},{2,4},{4,6},{6,8},{8,10},{10,12},{12,14},{14,0},{1,3},{3,5},... | collective-permute-start | bytes 589832 | tf_op jit(solution)/shard_map/ppermute | solution.py:167
  93.5 4.6 %collective-permute-start.8 = (bf16[16,16,384]{2,1,0:T(8,128)(2,1)S(1)}, bf16[16,16,384]{2,1,0:T(8,128)(2,1)S(1)}, u32[]{:S(2)}, u32[]{:S(2)}) collective-permute-start(bf16[16,16,384]{2,1,0:T(8,128)(2,1)S(1)} %slice.9), channel_id=1, source_target_pairs={{0,14},{2,0},{4,2},{6,4},{8,6},{10,8},{12,10},{14,12},{1,15},{3,1}... | collective-permute-start | bytes 589832 | tf_op jit(solution)/shard_map/ppermute | solution.py:168
  98.2 1.4 collective-permute-done.7.refs_4_
  100.6 14.1 %gram.1 = (f32[32,208,384]{2,1,0:T(8,128)}, f32[16,8,128]{2,1,0:T(8,128)S(1)}) custom-call(bf16[32,208,128]{2,1,0:T(8,128)(2,1)S(1)} %pad_maximum_fusion.cols_ref, bf16[32,16,384]{2,1,0:T(8,128)(2,1)S(1)} %bitcast.11, bf16[32,16,384]{2,1,0:T(8,128)(2,1)S(1)} %collective-permute-done.1.refs_1_, bf16[32,16,384]{2,1,0:T(8,128)(2,1)S(1)} %collective-permute-done.2.refs_2_, ...), custom_call_target="tpu_custom_call" | custom-call | tf_op jit(solution)/shard_map/gram/pallas_call | solution.py:190
  114.7 13.6 %all_to_all.25 = f32[16,8,128]{2,1,0:T(8,128)S(1)} all-to-all(f32[16,8,128]{2,1,0:T(8,128)S(1)} %get-tuple-element.9), channel_id=1, replica_groups=mesh['x'=4,'z'=8,'y'=8,'core'=2] {'z','core'}, dimensions={0} | all-to-all | bytes 131072 | tf_op jit(solution)/shard_map/all_to_all | solution.py:209
  128.4 17.4 %all_to_all.26.part_ref = f32[32,8,128]{2,1,0:T(8,128)} all-to-all(f32[32,8,128]{2,1,0:T(8,128)S(1)} %broadcast_in_dim.10), channel_id=1, replica_groups=mesh['x'=4,'z'=8,'y'=8,'core'=2] {'x','y'}, dimensions={0} | all-to-all | bytes 262144 | tf_op jit(solution)/shard_map/all_to_all | solution.py:211
  145.8 6.1 %combine.1 = (f32[384,128]{1,0:T(8,128)}, f32[384,128]{1,0:T(8,128)}) custom-call(f32[32,8,128]{2,1,0:T(8,128)} %all_to_all.26.part_ref, f32[32,208,384]{2,1,0:T(8,128)} %get-tuple-element.10.kept_ref), custom_call_target="tpu_custom_call" | custom-call | tf_op jit(solution)/shard_map/combine/pallas_call | solution.py:213
  151.9 4.1 %collective-permute-start.9 = (f32[384,128]{1,0:T(8,128)}, f32[384,128]{1,0:T(8,128)S(1)}, u32[]{:S(2)}, u32[]{:S(2)}) collective-permute-start(f32[384,128]{1,0:T(8,128)} %get-tuple-element.12), channel_id=1, source_target_pairs={{0,1},{1,0},{2,3},{3,2},{4,5},{5,4},{6,7},{7,6},{8,9},{9,8},{10,11... | collective-permute-start | bytes 589832 | tf_op jit(solution)/shard_map/ppermute | solution.py:229
  158.3 14.8 %all_to_all.27.pieces_ref = f32[32,24,128]{2,1,0:T(8,128)S(1)} all-to-all(f32[32,24,128]{2,1,0:T(8,128)S(1)} %bitcast.12), channel_id=1, replica_groups=mesh['x'=4,'z'=8,'y'=8,'core'=2] {'x','z'}, dimensions={0} | all-to-all | bytes 786432 | tf_op jit(solution)/shard_map/all_to_all | solution.py:233
  (20 shorter events, 4.8 us)
Async XLA Ops:
  0.0 16.4 %copy-start.1 = (bf16[128,3328]{1,0:T(8,128)(2,1)S(1)}, bf16[128,3328]{1,0:T(8,128)(2,1)}, u32[]{:S(2)}) copy-start(bf16[128,3328]{1,0:T(8,128)(2,1)} %param.4) | copy-start | bytes 2555908
  1.6 29.4 %all-to-all-start.1 = ((bf16[64,8,384]{2,1,0:T(8,128)(2,1)}), bf16[64,8,384]{2,1,0:T(8,128)(2,1)S(1)}, u32[]{:S(2)}, u32[]{:S(2)}) async-start(bf16[64,8,384]{2,1,0:T(8,128)(2,1)} %bitcast.4), calls=%async_computation.1 | async-start | bytes 786432 | tf_op jit(solution)/shard_map/all_to_all | solution.py:180
  31.0 26.1 %all-to-all-start = ((bf16[32,104,128]{2,1,0:T(8,128)(2,1)}), bf16[32,104,128]{2,1,0:T(8,128)(2,1)S(1)}, u32[]{:S(2)}, u32[]{:S(2)}) async-start(bf16[32,104,128]{2,1,0:T(8,128)(2,1)} %bitcast.1), calls=%async_computation | async-start | bytes 1703936 | tf_op jit(solution)/shard_map/all_to_all | solution.py:186
  36.2 27.6 %collective-permute-start.4 = (bf16[32,16,384]{2,1,0:T(8,128)(2,1)S(1)}, bf16[32,16,384]{2,1,0:T(8,128)(2,1)S(1)}, u32[]{:S(2)}, u32[]{:S(2)}) collective-permute-start(bf16[32,16,384]{2,1,0:T(8,128)(2,1)S(1)} %bitcast.9), channel_id=1, source_target_pairs={{0,2},{2,4},{4,6},{6,8},{8,10},{10,12},{12,14},{14,0},{1,3},{3,5},... | collective-permute-start | bytes 1179656 | tf_op jit(solution)/shard_map/ppermute | solution.py:167
  39.4 27.6 %collective-permute-start.1 = (bf16[32,16,384]{2,1,0:T(8,128)(2,1)S(1)}, bf16[32,16,384]{2,1,0:T(8,128)(2,1)S(1)}, u32[]{:S(2)}, u32[]{:S(2)}) collective-permute-start(bf16[32,16,384]{2,1,0:T(8,128)(2,1)S(1)} %bitcast.10), channel_id=1, source_target_pairs={{0,14},{2,0},{4,2},{6,4},{8,6},{10,8},{12,10},{14,12},{1,15},{3,1}... | collective-permute-start | bytes 1179656 | tf_op jit(solution)/shard_map/ppermute | solution.py:168
  57.1 40.9 %collective-permute-start = (bf16[32,104,128]{2,1,0:T(8,128)(2,1)S(1)}, bf16[32,104,128]{2,1,0:T(8,128)(2,1)S(1)}, u32[]{:S(2)}, u32[]{:S(2)}) collective-permute-start(bf16[32,104,128]{2,1,0:T(8,128)(2,1)S(1)} %all-to-all-done), channel_id=1, source_target_pairs={{0,1},{1,0},{2,3},{3,2},{4,5},{5,4},{6,7},{7,6},{8,9},{9,8},{10,11... | collective-permute-start | bytes 2555912 | tf_op jit(solution)/shard_map/ppermute | solution.py:187
  63.7 14.6 %collective-permute-start.5 = (bf16[32,16,384]{2,1,0:T(8,128)(2,1)S(1)}, bf16[32,16,384]{2,1,0:T(8,128)(2,1)S(1)}, u32[]{:S(2)}, u32[]{:S(2)}) collective-permute-start(bf16[32,16,384]{2,1,0:T(8,128)(2,1)S(1)} %collective-permute-done.4.refs_8_), channel_id=1, source_target_pairs={{0,2},{2,4},{4,6},{6,8},{8,10},{10,12},{12,14},{14,0},{1,3},{3,5},... | collective-permute-start | bytes 1179656 | tf_op jit(solution)/shard_map/ppermute | solution.py:167
  67.0 13.3 %collective-permute-start.2 = (bf16[32,16,384]{2,1,0:T(8,128)(2,1)S(1)}, bf16[32,16,384]{2,1,0:T(8,128)(2,1)S(1)}, u32[]{:S(2)}, u32[]{:S(2)}) collective-permute-start(bf16[32,16,384]{2,1,0:T(8,128)(2,1)S(1)} %collective-permute-done.1.refs_1_), channel_id=1, source_target_pairs={{0,14},{2,0},{4,2},{6,4},{8,6},{10,8},{12,10},{14,12},{1,15},{3,1}... | collective-permute-start | bytes 1179656 | tf_op jit(solution)/shard_map/ppermute | solution.py:168
  78.3 13.2 %collective-permute-start.6 = (bf16[32,16,384]{2,1,0:T(8,128)(2,1)S(1)}, bf16[32,16,384]{2,1,0:T(8,128)(2,1)S(1)}, u32[]{:S(2)}, u32[]{:S(2)}) collective-permute-start(bf16[32,16,384]{2,1,0:T(8,128)(2,1)S(1)} %collective-permute-done.5.refs_7_), channel_id=1, source_target_pairs={{0,2},{2,4},{4,6},{6,8},{8,10},{10,12},{12,14},{14,0},{1,3},{3,5},... | collective-permute-start | bytes 1179656 | tf_op jit(solution)/shard_map/ppermute | solution.py:167
  80.2 13.2 %collective-permute-start.3 = (bf16[32,16,384]{2,1,0:T(8,128)(2,1)S(1)}, bf16[32,16,384]{2,1,0:T(8,128)(2,1)S(1)}, u32[]{:S(2)}, u32[]{:S(2)}) collective-permute-start(bf16[32,16,384]{2,1,0:T(8,128)(2,1)S(1)} %collective-permute-done.2.refs_2_), channel_id=1, source_target_pairs={{0,14},{2,0},{4,2},{6,4},{8,6},{10,8},{12,10},{14,12},{1,15},{3,1}... | collective-permute-start | bytes 1179656 | tf_op jit(solution)/shard_map/ppermute | solution.py:168
  91.5 8.1 %collective-permute-start.7 = (bf16[16,16,384]{2,1,0:T(8,128)(2,1)S(1)}, bf16[16,16,384]{2,1,0:T(8,128)(2,1)S(1)}, u32[]{:S(2)}, u32[]{:S(2)}) collective-permute-start(bf16[16,16,384]{2,1,0:T(8,128)(2,1)S(1)} %slice.8), channel_id=1, source_target_pairs={{0,2},{2,4},{4,6},{6,8},{8,10},{10,12},{12,14},{14,0},{1,3},{3,5},... | collective-permute-start | bytes 589832 | tf_op jit(solution)/shard_map/ppermute | solution.py:167
  93.5 7.2 %collective-permute-start.8 = (bf16[16,16,384]{2,1,0:T(8,128)(2,1)S(1)}, bf16[16,16,384]{2,1,0:T(8,128)(2,1)S(1)}, u32[]{:S(2)}, u32[]{:S(2)}) collective-permute-start(bf16[16,16,384]{2,1,0:T(8,128)(2,1)S(1)} %slice.9), channel_id=1, source_target_pairs={{0,14},{2,0},{4,2},{6,4},{8,6},{10,8},{12,10},{14,12},{1,15},{3,1}... | collective-permute-start | bytes 589832 | tf_op jit(solution)/shard_map/ppermute | solution.py:168
  151.9 21.2 %copy-start = (f32[24,3328]{1,0:T(8,128)S(1)}, f32[24,3328]{1,0:T(8,128)}, u32[]{:S(2)}) copy-start(f32[24,3328]{1,0:T(8,128)} %momentum_ref.1) | copy-start | bytes 958468
  151.9 5.4 %collective-permute-start.9 = (f32[384,128]{1,0:T(8,128)}, f32[384,128]{1,0:T(8,128)S(1)}, u32[]{:S(2)}, u32[]{:S(2)}) collective-permute-start(f32[384,128]{1,0:T(8,128)} %get-tuple-element.12), channel_id=1, source_target_pairs={{0,1},{1,0},{2,3},{3,2},{4,5},{5,4},{6,7},{7,6},{8,9},{9,8},{10,11... | collective-permute-start | bytes 589832 | tf_op jit(solution)/shard_map/ppermute | solution.py:229
where the time goes:
time: 177 us; the launch traced here: 174 us
  starting transfers between devices  57.8 us (33%)
  blocking collectives  45.8 us (26%)
  waiting for transfers between devices  44.7 us (25%)
  Pallas kernels  21 us (12%)
  local copies, waits for them, and re-layouts  2.91 us (2%)
    all_to_all x1, blocking collectives, local(): lax.all_to_all(jnp.broadcast_to(gram, (32, 8, LANES)), ('x', 'y'), 0, 0,...  17.4 us
    ppermute x4, starting transfers between devices, ring(): above.append(lax.ppermute(from_above, 'y', down))  16.8 us
    ppermute x4, waiting for transfers between devices, ring(): below.append(lax.ppermute(from_below, 'y', up))  15.6 us
    all_to_all x1, starting transfers between devices, local(): halves = lax.all_to_all(halves, ('x', 'z', 'core'), 0, 0, tiled=True)  14.8 us
    all_to_all x1, blocking collectives, local(): pieces = lax.all_to_all(pieces, XZ, 0, 0, tiled=True)  14.8 us
    pallas_call x1, Pallas kernels, local(): pl.pallas_call(gram_kernel, out_shape=[jax.ShapeDtypeStruct((NR, 2 * shar...  14.1 us
    all_to_all x1, waiting for transfers between devices, local(): own = lax.all_to_all(rolled.T.reshape(NR, share, TOK), XZ, 0, 0, tiled=True)  13.9 us
    all_to_all x1, blocking collectives, local(): gram = lax.all_to_all(gram, ('z', 'core'), 0, 0, tiled=True)  13.6 us
  transfers between devices with their start and end apart: 12, of which 7 were waited for; matrix products, arithmetic and copies ran while one was open for 1% of the time, Pallas kernels for 0%

commit v1 on v0

--- a/solution.py
+++ b/solution.py
@@ -24,14 +24,12 @@
     unroll = 26
     assert groups % unroll == 0
 
-    opposite = len(act_refs) // 2
-    for r in range(NR):
-        half = r // (NR // 2)
-        parts = act_refs[:opposite] + act_refs[opposite + half : opposite + half + 1]
-        rows = [ref[r % ref.shape[0]] for ref in parts + act_refs[opposite + 2 :]]
-        act = jnp.concatenate(rows, axis=0)
+    def one(r, carry):
+        act = jnp.concatenate([ref[r] for ref in act_refs], axis=0)
         g_ref[r] = jnp.dot(cols_ref[r], act, preferred_element_type=jnp.float32)
-
+        return carry
+
+    lax.fori_loop(0, NR, one, 0, unroll=NR)
     save = pltpu.make_async_copy(g_ref, g_out_ref, sem)
     save.start()
     q_ref[...] = jnp.zeros_like(q_ref)
@@ -155,18 +153,14 @@
 
 def ring(block):
     size = lax.axis_size("y")
-    half = block.shape[0] // 2
     up = [(i, (i + 1) % size) for i in range(size)]
     down = [(i, (i - 1) % size) for i in range(size)]
     above, below = [block], [block]
     for step in range(size // 2):
-        last = step == size // 2 - 1
-        from_below, from_above = below[-1], above[-1]
-        if last:
-            from_below, from_above = from_below[:half], from_above[half:]
-        below.append(lax.ppermute(from_below, "y", up))
-        above.append(lax.ppermute(from_above, "y", down))
-    return above[:-1] + [below[-1], above[-1]] + below[-2:0:-1]
+        below.append(lax.ppermute(below[-1], "y", up))
+        if step < size // 2 - 1:
+            above.append(lax.ppermute(above[-1], "y", down))
+    return above + below[:0:-1]
 
 
 def local(activations, grad_out, momentum):
@@ -223,7 +217,7 @@
             pl.BlockSpec(memory_space=pltpu.VMEM),
             pl.BlockSpec(memory_space=pltpu.HBM),
         ],
-        compiler_params=pltpu.CompilerParams(vmem_limit_bytes=56 << 20),
+        compiler_params=pltpu.CompilerParams(vmem_limit_bytes=48 << 20),
         name="combine",
     )(gram, grads)
     came = lax.ppermute(theirs, "core", CORES)

time: 177 us -> 165 us (0.932)
  blocking collectives: 45.8 us -> 41.9 us
  starting transfers between devices: 57.8 us -> 53.9 us
  waiting for transfers between devices: 44.7 us -> 42.9 us
    all_to_all x1, waiting for transfers between devices: 13.9 us -> 5.32 us  [local(): own = lax.all_to_all(rolled.T.reshape(NR, share, TOK), XZ, 0, 0, tiled=True)]
    ppermute x8 -> x7, waiting for transfers between devices: 16.6 us -> 23.7 us  [the longest x3 12 us: ring(): above.append(lax.ppermute(above[-1], 'y', down))]
    ppermute x8 -> x7, starting transfers between devices: 27 us -> 23.2 us  [the longest x3 14.2 us: ring(): above.append(lax.ppermute(above[-1], 'y', down))]
    all_to_all x1, blocking collectives: 17.4 us -> 14.1 us  [local(): lax.all_to_all(jnp.broadcast_to(gram, (32, 8, LANES)), ('x', 'y'), 0, 0,...]
  transfers between devices with their start and end apart: 12 -> 11, of which waited for: 7 -> 7; matrix products, arithmetic and copies ran while one was open for 1% -> 1% of each run, Pallas kernels for 0% -> 0%
where the time goes in v1:
time: 165 us; the launch traced here: 162 us
  starting transfers between devices  53.9 us (33%)
  waiting for transfers between devices  42.9 us (26%)
  blocking collectives  41.9 us (25%)
  Pallas kernels  19.4 us (12%)
  local copies, waits for them, and re-layouts  2.85 us (2%)
    all_to_all x1, starting transfers between devices, local(): halves = lax.all_to_all(halves, ('x', 'z', 'core'), 0, 0, tiled=True)  14.8 us
    all_to_all x1, blocking collectives, local(): pieces = lax.all_to_all(pieces, XZ, 0, 0, tiled=True)  14.8 us
    ppermute x3, starting transfers between devices, ring(): above.append(lax.ppermute(above[-1], 'y', down))  14.2 us
    pallas_call x1, Pallas kernels, local(): pl.pallas_call(gram_kernel, out_shape=[jax.ShapeDtypeStruct((NR, 2 * shar...  14.1 us
    all_to_all x1, blocking collectives, local(): lax.all_to_all(jnp.broadcast_to(gram, (32, 8, LANES)), ('x', 'y'), 0, 0,...  14.1 us
    all_to_all x1, blocking collectives, local(): gram = lax.all_to_all(gram, ('z', 'core'), 0, 0, tiled=True)  13.1 us
    all_to_all x1, waiting for transfers between devices, local(): halves = lax.all_to_all(halves, ('x', 'z', 'core'), 0, 0, tiled=True)  12.9 us
    ppermute x3, waiting for transfers between devices, ring(): above.append(lax.ppermute(above[-1], 'y', down))  12 us
  transfers between devices with their start and end apart: 11, of which 7 were waited for; matrix products, arithmetic and copies ran while one was open for 1% of the time, Pallas kernels for 0%

profile of v1, /device:TPU:1, one launch (start us, length us, event | category | flops | bytes accessed | tf_op | source)
XLA Modules:
  0.0 161.8 jit_solution(10093263558092038079)
XLA Ops:
  0.0 1.6 broadcast_in_dim.4
  1.6 14.8 %all-to-all-start.1 = ((bf16[64,8,384]{2,1,0:T(8,128)(2,1)}), bf16[64,8,384]{2,1,0:T(8,128)(2,1)S(1)}, u32[]{:S(2)}, u32[]{:S(2)}) async-start(bf16[64,8,384]{2,1,0:T(8,128)(2,1)} %bitcast.4), calls=%async_computation.1 | async-start | bytes 786432 | tf_op jit(solution)/shard_map/all_to_all | solution.py:174
  16.9 1.2 copy.4
  18.1 12.9 %all-to-all-done.1 = bf16[64,8,384]{2,1,0:T(8,128)(2,1)S(1)} async-done(((bf16[64,8,384]{2,1,0:T(8,128)(2,1)}), bf16[64,8,384]{2,1,0:T(8,128)(2,1)S(1)}, u32[]{:S(2)}, u32[]{:S(2)}) %all-to-all-start.1) | async-done | bytes 393248 | tf_op jit(solution)/shard_map/all_to_all | solution.py:174
  31.0 5.2 %all-to-all-start = ((bf16[32,104,128]{2,1,0:T(8,128)(2,1)}), bf16[32,104,128]{2,1,0:T(8,128)(2,1)S(1)}, u32[]{:S(2)}, u32[]{:S(2)}) async-start(bf16[32,104,128]{2,1,0:T(8,128)(2,1)} %bitcast.1), calls=%async_computation | async-start | bytes 1703936 | tf_op jit(solution)/shard_map/all_to_all | solution.py:180
  36.2 3.2 %collective-permute-start.4 = (bf16[32,16,384]{2,1,0:T(8,128)(2,1)S(1)}, bf16[32,16,384]{2,1,0:T(8,128)(2,1)S(1)}, u32[]{:S(2)}, u32[]{:S(2)}) collective-permute-start(bf16[32,16,384]{2,1,0:T(8,128)(2,1)S(1)} %bitcast.9), channel_id=1, source_target_pairs={{0,2},{2,4},{4,6},{6,8},{8,10},{10,12},{12,14},{14,0},{1,3},{3,5},... | collective-permute-start | bytes 1179656 | tf_op jit(solution)/shard_map/ppermute | solution.py:160
  39.4 3.8 %collective-permute-start.1 = (bf16[32,16,384]{2,1,0:T(8,128)(2,1)S(1)}, bf16[32,16,384]{2,1,0:T(8,128)(2,1)S(1)}, u32[]{:S(2)}, u32[]{:S(2)}) collective-permute-start(bf16[32,16,384]{2,1,0:T(8,128)(2,1)S(1)} %bitcast.10), channel_id=1, source_target_pairs={{0,14},{2,0},{4,2},{6,4},{8,6},{10,8},{12,10},{14,12},{1,15},{3,1}... | collective-permute-start | bytes 1179656 | tf_op jit(solution)/shard_map/ppermute | solution.py:162
  43.2 6.7 %collective-permute-done.4.refs_7_ = bf16[32,16,384]{2,1,0:T(8,128)(2,1)S(1)} collective-permute-done((bf16[32,16,384]{2,1,0:T(8,128)(2,1)S(1)}, bf16[32,16,384]{2,1,0:T(8,128)(2,1)S(1)}, u32[]{:S(2)}, u32[]{:S(2)}) %collective-permute-start.4) | collective-permute-done | bytes 393248 | tf_op jit(solution)/shard_map/ppermute | solution.py:160
  49.9 1.9 %collective-permute-start.5 = (bf16[32,16,384]{2,1,0:T(8,128)(2,1)S(1)}, bf16[32,16,384]{2,1,0:T(8,128)(2,1)S(1)}, u32[]{:S(2)}, u32[]{:S(2)}) collective-permute-start(bf16[32,16,384]{2,1,0:T(8,128)(2,1)S(1)} %collective-permute-done.4.refs_7_), channel_id=1, source_target_pairs={{0,2},{2,4},{4,6},{6,8},{8,10},{10,12},{12,14},{14,0},{1,3},{3,5},... | collective-permute-start | bytes 1179656 | tf_op jit(solution)/shard_map/ppermute | solution.py:160
  51.8 5.3 %all-to-all-done = bf16[32,104,128]{2,1,0:T(8,128)(2,1)S(1)} async-done(((bf16[32,104,128]{2,1,0:T(8,128)(2,1)}), bf16[32,104,128]{2,1,0:T(8,128)(2,1)S(1)}, u32[]{:S(2)}, u32[]{:S(2)}) %all-to-all-start) | async-done | bytes 852000 | tf_op jit(solution)/shard_map/all_to_all | solution.py:180
  57.1 6.6 %collective-permute-start = (bf16[32,104,128]{2,1,0:T(8,128)(2,1)S(1)}, bf16[32,104,128]{2,1,0:T(8,128)(2,1)S(1)}, u32[]{:S(2)}, u32[]{:S(2)}) collective-permute-start(bf16[32,104,128]{2,1,0:T(8,128)(2,1)S(1)} %all-to-all-done), channel_id=1, source_target_pairs={{0,1},{1,0},{2,3},{3,2},{4,5},{5,4},{6,7},{7,6},{8,9},{9,8},{10,11... | collective-permute-start | bytes 2555912 | tf_op jit(solution)/shard_map/ppermute | solution.py:181
  63.7 5.1 %collective-permute-start.2 = (bf16[32,16,384]{2,1,0:T(8,128)(2,1)S(1)}, bf16[32,16,384]{2,1,0:T(8,128)(2,1)S(1)}, u32[]{:S(2)}, u32[]{:S(2)}) collective-permute-start(bf16[32,16,384]{2,1,0:T(8,128)(2,1)S(1)} %collective-permute-done.1.refs_1_), channel_id=1, source_target_pairs={{0,14},{2,0},{4,2},{6,4},{8,6},{10,8},{12,10},{14,12},{1,15},{3,1}... | collective-permute-start | bytes 1179656 | tf_op jit(solution)/shard_map/ppermute | solution.py:162
  68.8 1.9 %collective-permute-start.6 = (bf16[32,16,384]{2,1,0:T(8,128)(2,1)S(1)}, bf16[32,16,384]{2,1,0:T(8,128)(2,1)S(1)}, u32[]{:S(2)}, u32[]{:S(2)}) collective-permute-start(bf16[32,16,384]{2,1,0:T(8,128)(2,1)S(1)} %collective-permute-done.5.refs_6_), channel_id=1, source_target_pairs={{0,2},{2,4},{4,6},{6,8},{8,10},{10,12},{12,14},{14,0},{1,3},{3,5},... | collective-permute-start | bytes 1179656 | tf_op jit(solution)/shard_map/ppermute | solution.py:160
  70.8 6.5 %collective-permute-done.2.refs_2_ = bf16[32,16,384]{2,1,0:T(8,128)(2,1)S(1)} collective-permute-done((bf16[32,16,384]{2,1,0:T(8,128)(2,1)S(1)}, bf16[32,16,384]{2,1,0:T(8,128)(2,1)S(1)}, u32[]{:S(2)}, u32[]{:S(2)}) %collective-permute-start.2) | collective-permute-done | bytes 393248 | tf_op jit(solution)/shard_map/ppermute | solution.py:162
  77.3 5.3 %collective-permute-start.3 = (bf16[32,16,384]{2,1,0:T(8,128)(2,1)S(1)}, bf16[32,16,384]{2,1,0:T(8,128)(2,1)S(1)}, u32[]{:S(2)}, u32[]{:S(2)}) collective-permute-start(bf16[32,16,384]{2,1,0:T(8,128)(2,1)S(1)} %collective-permute-done.2.refs_2_), channel_id=1, source_target_pairs={{0,14},{2,0},{4,2},{6,4},{8,6},{10,8},{12,10},{14,12},{1,15},{3,1}... | collective-permute-start | bytes 1179656 | tf_op jit(solution)/shard_map/ppermute | solution.py:162
  82.6 1.9 %collective-permute-start.7 = (bf16[32,16,384]{2,1,0:T(8,128)(2,1)S(1)}, bf16[32,16,384]{2,1,0:T(8,128)(2,1)S(1)}, u32[]{:S(2)}, u32[]{:S(2)}) collective-permute-start(bf16[32,16,384]{2,1,0:T(8,128)(2,1)S(1)} %collective-permute-done.6.refs_5_), channel_id=1, source_target_pairs={{0,2},{2,4},{4,6},{6,8},{8,10},{10,12},{12,14},{14,0},{1,3},{3,5},... | collective-permute-start | bytes 1179656 | tf_op jit(solution)/shard_map/ppermute | solution.py:160
  84.7 5.5 %collective-permute-done.3.refs_3_ = bf16[32,16,384]{2,1,0:T(8,128)(2,1)S(1)} collective-permute-done((bf16[32,16,384]{2,1,0:T(8,128)(2,1)S(1)}, bf16[32,16,384]{2,1,0:T(8,128)(2,1)S(1)}, u32[]{:S(2)}, u32[]{:S(2)}) %collective-permute-start.3) | collective-permute-done | bytes 393248 | tf_op jit(solution)/shard_map/ppermute | solution.py:162
  90.2 5.1 %collective-permute-done.7.refs_4_ = bf16[32,16,384]{2,1,0:T(8,128)(2,1)S(1)} collective-permute-done((bf16[32,16,384]{2,1,0:T(8,128)(2,1)S(1)}, bf16[32,16,384]{2,1,0:T(8,128)(2,1)S(1)}, u32[]{:S(2)}, u32[]{:S(2)}) %collective-permute-start.7) | collective-permute-done | bytes 393248 | tf_op jit(solution)/shard_map/ppermute | solution.py:160
  95.2 14.1 %gram.1 = (f32[32,208,384]{2,1,0:T(8,128)}, f32[16,8,128]{2,1,0:T(8,128)S(1)}) custom-call(bf16[32,208,128]{2,1,0:T(8,128)(2,1)S(1)} %pad_maximum_fusion.cols_ref, bf16[32,16,384]{2,1,0:T(8,128)(2,1)S(1)} %bitcast.11, bf16[32,16,384]{2,1,0:T(8,128)(2,1)S(1)} %collective-permute-done.1.refs_1_, bf16[32,16,384]{2,1,0:T(8,128)(2,1)S(1)} %collective-permute-done.2.refs_2_, ...), custom_call_target="tpu_custom_call" | custom-call | tf_op jit(solution)/shard_map/gram/pallas_call | solution.py:184
  109.3 13.1 %all_to_all.25 = f32[16,8,128]{2,1,0:T(8,128)S(1)} all-to-all(f32[16,8,128]{2,1,0:T(8,128)S(1)} %get-tuple-element.9), channel_id=1, replica_groups=mesh['x'=4,'z'=8,'y'=8,'core'=2] {'z','core'}, dimensions={0} | all-to-all | bytes 131072 | tf_op jit(solution)/shard_map/all_to_all | solution.py:203
  122.4 14.1 %all_to_all.26.part_ref = f32[32,8,128]{2,1,0:T(8,128)S(1)} all-to-all(f32[32,8,128]{2,1,0:T(8,128)S(1)} %broadcast_in_dim.10), channel_id=1, replica_groups=mesh['x'=4,'z'=8,'y'=8,'core'=2] {'x','y'}, dimensions={0} | all-to-all | bytes 262144 | tf_op jit(solution)/shard_map/all_to_all | solution.py:205
  136.5 4.4 %combine.1 = (f32[384,128]{1,0:T(8,128)S(1)}, f32[384,128]{1,0:T(8,128)S(1)}) custom-call(f32[32,8,128]{2,1,0:T(8,128)S(1)} %all_to_all.26.part_ref, f32[32,208,384]{2,1,0:T(8,128)} %get-tuple-element.10.kept_ref), custom_call_target="tpu_custom_call" | custom-call | tf_op jit(solution)/shard_map/combine/pallas_call | solution.py:207
  140.9 4.2 %collective-permute-start.8 = (f32[384,128]{1,0:T(8,128)S(1)}, f32[384,128]{1,0:T(8,128)S(1)}, u32[]{:S(2)}, u32[]{:S(2)}) collective-permute-start(f32[384,128]{1,0:T(8,128)S(1)} %get-tuple-element.12), channel_id=1, source_target_pairs={{0,1},{1,0},{2,3},{3,2},{4,5},{5,4},{6,7},{7,6},{8,9},{9,8},{10,11... | collective-permute-start | bytes 589832 | tf_op jit(solution)/shard_map/ppermute | solution.py:223
  146.2 14.8 %all_to_all.27.pieces_ref = f32[32,24,128]{2,1,0:T(8,128)S(1)} all-to-all(f32[32,24,128]{2,1,0:T(8,128)S(1)} %bitcast.12), channel_id=1, replica_groups=mesh['x'=4,'z'=8,'y'=8,'core'=2] {'x','z'}, dimensions={0} | all-to-all | bytes 786432 | tf_op jit(solution)/shard_map/all_to_all | solution.py:227
  (16 shorter events, 2.6 us)
Async XLA Ops:
  0.0 16.4 %copy-start.1 = (bf16[128,3328]{1,0:T(8,128)(2,1)S(1)}, bf16[128,3328]{1,0:T(8,128)(2,1)}, u32[]{:S(2)}) copy-start(bf16[128,3328]{1,0:T(8,128)(2,1)} %param.4) | copy-start | bytes 2555908
  1.6 29.4 %all-to-all-start.1 = ((bf16[64,8,384]{2,1,0:T(8,128)(2,1)}), bf16[64,8,384]{2,1,0:T(8,128)(2,1)S(1)}, u32[]{:S(2)}, u32[]{:S(2)}) async-start(bf16[64,8,384]{2,1,0:T(8,128)(2,1)} %bitcast.4), calls=%async_computation.1 | async-start | bytes 786432 | tf_op jit(solution)/shard_map/all_to_all | solution.py:174
  31.0 26.1 %all-to-all-start = ((bf16[32,104,128]{2,1,0:T(8,128)(2,1)}), bf16[32,104,128]{2,1,0:T(8,128)(2,1)S(1)}, u32[]{:S(2)}, u32[]{:S(2)}) async-start(bf16[32,104,128]{2,1,0:T(8,128)(2,1)} %bitcast.1), calls=%async_computation | async-start | bytes 1703936 | tf_op jit(solution)/shard_map/all_to_all | solution.py:180
  36.2 13.7 %collective-permute-start.4 = (bf16[32,16,384]{2,1,0:T(8,128)(2,1)S(1)}, bf16[32,16,384]{2,1,0:T(8,128)(2,1)S(1)}, u32[]{:S(2)}, u32[]{:S(2)}) collective-permute-start(bf16[32,16,384]{2,1,0:T(8,128)(2,1)S(1)} %bitcast.9), channel_id=1, source_target_pairs={{0,2},{2,4},{4,6},{6,8},{8,10},{10,12},{12,14},{14,0},{1,3},{3,5},... | collective-permute-start | bytes 1179656 | tf_op jit(solution)/shard_map/ppermute | solution.py:160
  39.4 24.3 %collective-permute-start.1 = (bf16[32,16,384]{2,1,0:T(8,128)(2,1)S(1)}, bf16[32,16,384]{2,1,0:T(8,128)(2,1)S(1)}, u32[]{:S(2)}, u32[]{:S(2)}) collective-permute-start(bf16[32,16,384]{2,1,0:T(8,128)(2,1)S(1)} %bitcast.10), channel_id=1, source_target_pairs={{0,14},{2,0},{4,2},{6,4},{8,6},{10,8},{12,10},{14,12},{1,15},{3,1}... | collective-permute-start | bytes 1179656 | tf_op jit(solution)/shard_map/ppermute | solution.py:162
  49.9 19.0 %collective-permute-start.5 = (bf16[32,16,384]{2,1,0:T(8,128)(2,1)S(1)}, bf16[32,16,384]{2,1,0:T(8,128)(2,1)S(1)}, u32[]{:S(2)}, u32[]{:S(2)}) collective-permute-start(bf16[32,16,384]{2,1,0:T(8,128)(2,1)S(1)} %collective-permute-done.4.refs_7_), channel_id=1, source_target_pairs={{0,2},{2,4},{4,6},{6,8},{8,10},{10,12},{12,14},{14,0},{1,3},{3,5},... | collective-permute-start | bytes 1179656 | tf_op jit(solution)/shard_map/ppermute | solution.py:160
  57.1 27.4 %collective-permute-start = (bf16[32,104,128]{2,1,0:T(8,128)(2,1)S(1)}, bf16[32,104,128]{2,1,0:T(8,128)(2,1)S(1)}, u32[]{:S(2)}, u32[]{:S(2)}) collective-permute-start(bf16[32,104,128]{2,1,0:T(8,128)(2,1)S(1)} %all-to-all-done), channel_id=1, source_target_pairs={{0,1},{1,0},{2,3},{3,2},{4,5},{5,4},{6,7},{7,6},{8,9},{9,8},{10,11... | collective-permute-start | bytes 2555912 | tf_op jit(solution)/shard_map/ppermute | solution.py:181
  63.7 13.5 %collective-permute-start.2 = (bf16[32,16,384]{2,1,0:T(8,128)(2,1)S(1)}, bf16[32,16,384]{2,1,0:T(8,128)(2,1)S(1)}, u32[]{:S(2)}, u32[]{:S(2)}) collective-permute-start(bf16[32,16,384]{2,1,0:T(8,128)(2,1)S(1)} %collective-permute-done.1.refs_1_), channel_id=1, source_target_pairs={{0,14},{2,0},{4,2},{6,4},{8,6},{10,8},{12,10},{14,12},{1,15},{3,1}... | collective-permute-start | bytes 1179656 | tf_op jit(solution)/shard_map/ppermute | solution.py:162
  68.8 13.7 %collective-permute-start.6 = (bf16[32,16,384]{2,1,0:T(8,128)(2,1)S(1)}, bf16[32,16,384]{2,1,0:T(8,128)(2,1)S(1)}, u32[]{:S(2)}, u32[]{:S(2)}) collective-permute-start(bf16[32,16,384]{2,1,0:T(8,128)(2,1)S(1)} %collective-permute-done.5.refs_6_), channel_id=1, source_target_pairs={{0,2},{2,4},{4,6},{6,8},{8,10},{10,12},{12,14},{14,0},{1,3},{3,5},... | collective-permute-start | bytes 1179656 | tf_op jit(solution)/shard_map/ppermute | solution.py:160
  77.3 12.9 %collective-permute-start.3 = (bf16[32,16,384]{2,1,0:T(8,128)(2,1)S(1)}, bf16[32,16,384]{2,1,0:T(8,128)(2,1)S(1)}, u32[]{:S(2)}, u32[]{:S(2)}) collective-permute-start(bf16[32,16,384]{2,1,0:T(8,128)(2,1)S(1)} %collective-permute-done.2.refs_2_), channel_id=1, source_target_pairs={{0,14},{2,0},{4,2},{6,4},{8,6},{10,8},{12,10},{14,12},{1,15},{3,1}... | collective-permute-start | bytes 1179656 | tf_op jit(solution)/shard_map/ppermute | solution.py:162
  82.6 12.6 %collective-permute-start.7 = (bf16[32,16,384]{2,1,0:T(8,128)(2,1)S(1)}, bf16[32,16,384]{2,1,0:T(8,128)(2,1)S(1)}, u32[]{:S(2)}, u32[]{:S(2)}) collective-permute-start(bf16[32,16,384]{2,1,0:T(8,128)(2,1)S(1)} %collective-permute-done.6.refs_5_), channel_id=1, source_target_pairs={{0,2},{2,4},{4,6},{6,8},{8,10},{10,12},{12,14},{14,0},{1,3},{3,5},... | collective-permute-start | bytes 1179656 | tf_op jit(solution)/shard_map/ppermute | solution.py:160
  140.9 20.0 %copy-start = (f32[24,3328]{1,0:T(8,128)S(1)}, f32[24,3328]{1,0:T(8,128)}, u32[]{:S(2)}) copy-start(f32[24,3328]{1,0:T(8,128)} %momentum_ref.1) | copy-start | bytes 958468
  140.9 5.2 %collective-permute-start.8 = (f32[384,128]{1,0:T(8,128)S(1)}, f32[384,128]{1,0:T(8,128)S(1)}, u32[]{:S(2)}, u32[]{:S(2)}) collective-permute-start(f32[384,128]{1,0:T(8,128)S(1)} %get-tuple-element.12), channel_id=1, source_target_pairs={{0,1},{1,0},{2,3},{3,2},{4,5},{5,4},{6,7},{7,6},{8,9},{9,8},{10,11... | collective-permute-start | bytes 589832 | tf_op jit(solution)/shard_map/ppermute | solution.py:223

commit v2 on v1

--- a/solution.py
+++ b/solution.py
@@ -13,11 +13,11 @@
 LANES = 128
 XZ = ("x", "z")
 CORES = [(0, 1), (1, 0)]
-PIECES = ((0, 56), (56, 56), (112, 56), (168, 40))
+PIECES = ((0, 56), (56, 48))
 
 
 def gram_kernel(cols_ref, *refs):
-    act_refs, (g_out_ref, gram_ref, g_ref, q_ref, sem) = refs[:-5], refs[-5:]
+    act_refs, outs, (gram_ref, g_ref, q_ref, sem) = refs[:-6], refs[-6:-4], refs[-4:]
     groups = cols_ref.shape[1] // 8
     depth = act_refs[0].shape[-1]
     lane_blocks = depth // LANES
@@ -30,8 +30,11 @@
         return carry
 
     lax.fori_loop(0, NR, one, 0, unroll=NR)
-    save = pltpu.make_async_copy(g_ref, g_out_ref, sem)
-    save.start()
+    saves = []
+    for part, out in enumerate(outs):
+        rows = pl.ds(part * out.shape[1], out.shape[1])
+        saves.append(pltpu.make_async_copy(g_ref.at[:, rows], out, sem.at[part]))
+        saves[-1].start()
     q_ref[...] = jnp.zeros_like(q_ref)
 
     def pair_block(rb, sb, same):
@@ -79,7 +82,8 @@
         row = sums[i : i + 1, i * LANES : (i + 1) * LANES]
         for k in range(gram_ref.shape[0]):
             gram_ref[k, i : i + 1, :] = row
-    save.wait()
+    for save in saves:
+        save.wait()
 
 
 def tree_weights(packed):
@@ -111,38 +115,50 @@
     return w_col
 
 
-def combine_kernel(part_ref, kept_ref, mine_ref, theirs_ref, w_ref, ct_ref, g_ref, sem):
-    share = kept_ref.shape[1] // 2
-    lane_blocks = kept_ref.shape[2] // LANES
+def combine_kernel(core_ref, part_ref, own_ref, came_ref, out_ref, w_ref, ct_ref, g_ref, sem):
+    core = core_ref[0]
+    share = own_ref.shape[1]
+    lane_blocks = own_ref.shape[2] // LANES
     loads = []
-    for k, (start, size) in enumerate(PIECES):
-        rows = pl.ds(start, size)
-        loads.append(pltpu.make_async_copy(kept_ref.at[:, rows], g_ref.at[:, rows], sem.at[k]))
-        loads[-1].start()
+    for part, ref in enumerate((own_ref, came_ref)):
+        for k, (start, size) in enumerate(PIECES):
+            rows = pl.ds(start, size)
+            loads.append(
+                pltpu.make_async_copy(
+                    ref.at[:, rows], g_ref.at[part, :, rows], sem.at[part * len(PIECES) + k]
+                )
+            )
+            loads[-1].start()
     weights = tree_weights(jnp.sum(part_ref[...], axis=0))
     for r in range(NR):
         w_ref[r] = jnp.broadcast_to(weights[r : r + 1, :], (8, LANES))
-    ct_ref[pl.ds(2 * share, 48), :] = jnp.zeros((48, ct_ref.shape[1]), jnp.float32)
-
-    def body(f, carry):
+
+    def add_up(part, f):
         row = pl.multiple_of(f * 8, 8)
         acc = [None] * lane_blocks
         for r in range(NR):
             weight = w_ref[r]
             for k in range(lane_blocks):
-                term = g_ref[r, pl.ds(row, 8), k * LANES : (k + 1) * LANES] * weight
+                term = g_ref[part, r, pl.ds(row, 8), k * LANES : (k + 1) * LANES] * weight
                 acc[k] = term if r == 0 else acc[k] + term
         for k in range(lane_blocks):
-            ct_ref[pl.ds(row, 8), k * LANES : (k + 1) * LANES] = acc[k]
-        return carry
-
-    for load, (start, size) in zip(loads, PIECES):
-        load.wait()
-        lax.fori_loop(start // 8, (start + size) // 8, body, 0)
-    for part, ref in enumerate((mine_ref, theirs_ref)):
+            ct_ref[part, pl.ds(row, 8), k * LANES : (k + 1) * LANES] = acc[k]
+
+    for part in range(2):
+        tail = ct_ref.shape[1] - share
+        ct_ref[part, pl.ds(share, tail), :] = jnp.zeros((tail, ct_ref.shape[2]), jnp.float32)
+        for k, (start, size) in enumerate(PIECES):
+            loads[part * len(PIECES) + k].wait()
+
+            def body(f, carry):
+                add_up(part, f)
+                return carry
+
+            lax.fori_loop(start // 8, (start + size) // 8, body, 0)
+        place = core if part == 0 else 1 - core
         for k in range(lane_blocks):
             lanes = slice(k * LANES, (k + 1) * LANES)
-            ref[lanes, :] = ct_ref[share * part : share * part + LANES, lanes].T
+            out_ref[place, lanes, :] = ct_ref[part, :, lanes].T
 
 
 def finish_kernel(pieces_ref, momentum_ref, out_ref):
@@ -181,49 +197,51 @@
     other = lax.ppermute(own, "core", CORES)
     cols = jnp.concatenate([own, other], axis=1)
 
-    grads, gram = pl.pallas_call(
+    grads, to_swap, gram = pl.pallas_call(
         gram_kernel,
         out_shape=[
-            jax.ShapeDtypeStruct((NR, 2 * share, depth), jnp.float32),
+            jax.ShapeDtypeStruct((NR, share, depth), jnp.float32),
+            jax.ShapeDtypeStruct((NR, share, depth), jnp.float32),
             jax.ShapeDtypeStruct((16, 8, LANES), jnp.float32),
         ],
         out_specs=[
+            pl.BlockSpec(memory_space=pltpu.HBM),
             pl.BlockSpec(memory_space=pltpu.HBM),
             pl.BlockSpec(memory_space=pltpu.VMEM),
         ],
         scratch_shapes=[
             pltpu.VMEM((NR, 2 * share, depth), jnp.float32),
             pltpu.VMEM((1024, LANES), jnp.float32),
-            pltpu.SemaphoreType.DMA,
+            pltpu.SemaphoreType.DMA((2,)),
         ],
         compiler_params=pltpu.CompilerParams(vmem_limit_bytes=48 << 20),
         name="gram",
     )(cols, *acts)
 
     gram = lax.all_to_all(gram, ("z", "core"), 0, 0, tiled=True)
+    came = lax.ppermute(to_swap, "core", CORES)
     gram = jnp.sum(gram, axis=0)
     gram = lax.all_to_all(jnp.broadcast_to(gram, (32, 8, LANES)), ("x", "y"), 0, 0, tiled=True)
 
-    mine, theirs = pl.pallas_call(
+    pieces = pl.pallas_call(
         combine_kernel,
-        out_shape=[jax.ShapeDtypeStruct((depth, LANES), jnp.float32)] * 2,
+        out_shape=jax.ShapeDtypeStruct((2, depth, LANES), jnp.float32),
         scratch_shapes=[
             pltpu.VMEM((NR, 8, LANES), jnp.float32),
-            pltpu.VMEM((256, depth), jnp.float32),
-            pltpu.VMEM(grads.shape, jnp.float32),
-            pltpu.SemaphoreType.DMA((len(PIECES),)),
+            pltpu.VMEM((2, LANES, depth), jnp.float32),
+            pltpu.VMEM((2, NR, share, depth), jnp.float32),
+            pltpu.SemaphoreType.DMA((2 * len(PIECES),)),
         ],
         in_specs=[
+            pl.BlockSpec(memory_space=pltpu.SMEM),
             pl.BlockSpec(memory_space=pltpu.VMEM),
             pl.BlockSpec(memory_space=pltpu.HBM),
-        ],
-        compiler_params=pltpu.CompilerParams(vmem_limit_bytes=48 << 20),
+            pl.BlockSpec(memory_space=pltpu.HBM),
+        ],
+        compiler_params=pltpu.CompilerParams(vmem_limit_bytes=52 << 20),
         name="combine",
-    )(gram, grads)
-    came = lax.ppermute(theirs, "core", CORES)
-    low = jnp.where(core == 0, mine, came)
-    high = jnp.where(core == 0, came, mine)
-    pieces = jnp.concatenate([low, high], axis=0).reshape(NR, 24, LANES)
+    )(core.astype(jnp.int32).reshape(1), gram, grads, came)
+    pieces = pieces.reshape(NR, 24, LANES)
     pieces = lax.all_to_all(pieces, XZ, 0, 0, tiled=True)
 
     return pl.pallas_call(

time: 165 us -> 163 us (0.988)
  the two profiles are of different devices: /device:TPU:1 before, /device:TPU:8 now
where the time goes in v2:
time: 163 us; the launch traced here: 162 us
  waiting for transfers between devices  58.1 us (36%)
  starting transfers between devices  51.9 us (32%)
  blocking collectives  28.3 us (17%)
  Pallas kernels  19.5 us (12%)
  local copies, waits for them, and re-layouts  3.5 us (2%)
    all_to_all x1, blocking collectives, local(): pieces = lax.all_to_all(pieces, XZ, 0, 0, tiled=True)  17 us
    pallas_call x1, Pallas kernels, local(): pl.pallas_call(gram_kernel, out_shape=[jax.ShapeDtypeStruct((NR, share, d...  14.2 us
    ppermute x3, waiting for transfers between devices, ring(): above.append(lax.ppermute(above[-1], 'y', down))  14.1 us
    all_to_all x1, starting transfers between devices, local(): halves = lax.all_to_all(halves, ('x', 'z', 'core'), 0, 0, tiled=True)  13.8 us
    all_to_all x1, waiting for transfers between devices, local(): halves = lax.all_to_all(halves, ('x', 'z', 'core'), 0, 0, tiled=True)  12.8 us
    ppermute x4, starting transfers between devices, ring(): below.append(lax.ppermute(below[-1], 'y', up))  12.5 us
    ppermute x4, waiting for transfers between devices, ring(): below.append(lax.ppermute(below[-1], 'y', up))  12.2 us
    all_to_all x1, blocking collectives, local(): gram = lax.all_to_all(gram, ('z', 'core'), 0, 0, tiled=True)  11.3 us
  transfers between devices with their start and end apart: 12, of which 8 were waited for; matrix products, arithmetic and copies ran while one was open for 2% of the time, Pallas kernels for 0%

profile of v2, /device:TPU:8, one launch (start us, length us, event | category | flops | bytes accessed | tf_op | source)
XLA Modules:
  0.0 162.1 jit_solution(3618189980439995104)
XLA Ops:
  0.0 1.6 broadcast_in_dim.4
  1.6 13.8 %all-to-all-start.1 = ((bf16[64,8,384]{2,1,0:T(8,128)(2,1)}), bf16[64,8,384]{2,1,0:T(8,128)(2,1)S(1)}, u32[]{:S(2)}, u32[]{:S(2)}) async-start(bf16[64,8,384]{2,1,0:T(8,128)(2,1)} %bitcast.5), calls=%async_computation.1 | async-start | bytes 786432 | tf_op jit(solution)/shard_map/all_to_all | solution.py:190
  17.1 12.8 %all-to-all-done.1 = bf16[64,8,384]{2,1,0:T(8,128)(2,1)S(1)} async-done(((bf16[64,8,384]{2,1,0:T(8,128)(2,1)}), bf16[64,8,384]{2,1,0:T(8,128)(2,1)S(1)}, u32[]{:S(2)}, u32[]{:S(2)}) %all-to-all-start.1) | async-done | bytes 393248 | tf_op jit(solution)/shard_map/all_to_all | solution.py:190
  29.9 5.7 %all-to-all-start = ((bf16[32,104,128]{2,1,0:T(8,128)(2,1)}), bf16[32,104,128]{2,1,0:T(8,128)(2,1)S(1)}, u32[]{:S(2)}, u32[]{:S(2)}) async-start(bf16[32,104,128]{2,1,0:T(8,128)(2,1)} %bitcast.2), calls=%async_computation | async-start | bytes 1703936 | tf_op jit(solution)/shard_map/all_to_all | solution.py:196
  35.5 3.5 %collective-permute-start.4 = (bf16[32,16,384]{2,1,0:T(8,128)(2,1)S(1)}, bf16[32,16,384]{2,1,0:T(8,128)(2,1)S(1)}, u32[]{:S(2)}, u32[]{:S(2)}) collective-permute-start(bf16[32,16,384]{2,1,0:T(8,128)(2,1)S(1)} %bitcast.11), channel_id=1, source_target_pairs={{0,2},{2,4},{4,6},{6,8},{8,10},{10,12},{12,14},{14,0},{1,3},{3,5},... | collective-permute-start | bytes 1179656 | tf_op jit(solution)/shard_map/ppermute | solution.py:176
  39.0 2.4 %collective-permute-start.1 = (bf16[32,16,384]{2,1,0:T(8,128)(2,1)S(1)}, bf16[32,16,384]{2,1,0:T(8,128)(2,1)S(1)}, u32[]{:S(2)}, u32[]{:S(2)}) collective-permute-start(bf16[32,16,384]{2,1,0:T(8,128)(2,1)S(1)} %bitcast.12), channel_id=1, source_target_pairs={{0,14},{2,0},{4,2},{6,4},{8,6},{10,8},{12,10},{14,12},{1,15},{3,1}... | collective-permute-start | bytes 1179656 | tf_op jit(solution)/shard_map/ppermute | solution.py:178
  41.4 6.7 %collective-permute-done.4.refs_7_ = bf16[32,16,384]{2,1,0:T(8,128)(2,1)S(1)} collective-permute-done((bf16[32,16,384]{2,1,0:T(8,128)(2,1)S(1)}, bf16[32,16,384]{2,1,0:T(8,128)(2,1)S(1)}, u32[]{:S(2)}, u32[]{:S(2)}) %collective-permute-start.4) | collective-permute-done | bytes 393248 | tf_op jit(solution)/shard_map/ppermute | solution.py:176
  48.1 3.5 %collective-permute-start.5 = (bf16[32,16,384]{2,1,0:T(8,128)(2,1)S(1)}, bf16[32,16,384]{2,1,0:T(8,128)(2,1)S(1)}, u32[]{:S(2)}, u32[]{:S(2)}) collective-permute-start(bf16[32,16,384]{2,1,0:T(8,128)(2,1)S(1)} %collective-permute-done.4.refs_7_), channel_id=1, source_target_pairs={{0,2},{2,4},{4,6},{6,8},{8,10},{10,12},{12,14},{14,0},{1,3},{3,5},... | collective-permute-start | bytes 1179656 | tf_op jit(solution)/shard_map/ppermute | solution.py:176
  51.6 8.7 %all-to-all-done = bf16[32,104,128]{2,1,0:T(8,128)(2,1)S(1)} async-done(((bf16[32,104,128]{2,1,0:T(8,128)(2,1)}), bf16[32,104,128]{2,1,0:T(8,128)(2,1)S(1)}, u32[]{:S(2)}, u32[]{:S(2)}) %all-to-all-start) | async-done | bytes 852000 | tf_op jit(solution)/shard_map/all_to_all | solution.py:196
  60.3 1.9 %collective-permute-start = (bf16[32,104,128]{2,1,0:T(8,128)(2,1)S(1)}, bf16[32,104,128]{2,1,0:T(8,128)(2,1)S(1)}, u32[]{:S(2)}, u32[]{:S(2)}) collective-permute-start(bf16[32,104,128]{2,1,0:T(8,128)(2,1)S(1)} %all-to-all-done), channel_id=1, source_target_pairs={{0,1},{1,0},{2,3},{3,2},{4,5},{5,4},{6,7},{7,6},{8,9},{9,8},{10,11... | collective-permute-start | bytes 2555912 | tf_op jit(solution)/shard_map/ppermute | solution.py:197
  62.2 2.4 %collective-permute-start.2 = (bf16[32,16,384]{2,1,0:T(8,128)(2,1)S(1)}, bf16[32,16,384]{2,1,0:T(8,128)(2,1)S(1)}, u32[]{:S(2)}, u32[]{:S(2)}) collective-permute-start(bf16[32,16,384]{2,1,0:T(8,128)(2,1)S(1)} %collective-permute-done.1.refs_1_), channel_id=1, source_target_pairs={{0,14},{2,0},{4,2},{6,4},{8,6},{10,8},{12,10},{14,12},{1,15},{3,1}... | collective-permute-start | bytes 1179656 | tf_op jit(solution)/shard_map/ppermute | solution.py:178
  64.6 3.5 %collective-permute-start.6 = (bf16[32,16,384]{2,1,0:T(8,128)(2,1)S(1)}, bf16[32,16,384]{2,1,0:T(8,128)(2,1)S(1)}, u32[]{:S(2)}, u32[]{:S(2)}) collective-permute-start(bf16[32,16,384]{2,1,0:T(8,128)(2,1)S(1)} %collective-permute-done.5.refs_6_), channel_id=1, source_target_pairs={{0,2},{2,4},{4,6},{6,8},{8,10},{10,12},{12,14},{14,0},{1,3},{3,5},... | collective-permute-start | bytes 1179656 | tf_op jit(solution)/shard_map/ppermute | solution.py:176
  68.1 7.5 %collective-permute-done.2.refs_2_ = bf16[32,16,384]{2,1,0:T(8,128)(2,1)S(1)} collective-permute-done((bf16[32,16,384]{2,1,0:T(8,128)(2,1)S(1)}, bf16[32,16,384]{2,1,0:T(8,128)(2,1)S(1)}, u32[]{:S(2)}, u32[]{:S(2)}) %collective-permute-start.2) | collective-permute-done | bytes 393248 | tf_op jit(solution)/shard_map/ppermute | solution.py:178
  75.7 3.3 %collective-permute-start.3 = (bf16[32,16,384]{2,1,0:T(8,128)(2,1)S(1)}, bf16[32,16,384]{2,1,0:T(8,128)(2,1)S(1)}, u32[]{:S(2)}, u32[]{:S(2)}) collective-permute-start(bf16[32,16,384]{2,1,0:T(8,128)(2,1)S(1)} %collective-permute-done.2.refs_2_), channel_id=1, source_target_pairs={{0,14},{2,0},{4,2},{6,4},{8,6},{10,8},{12,10},{14,12},{1,15},{3,1}... | collective-permute-start | bytes 1179656 | tf_op jit(solution)/shard_map/ppermute | solution.py:178
  79.5 2.0 %collective-permute-start.7 = (bf16[32,16,384]{2,1,0:T(8,128)(2,1)S(1)}, bf16[32,16,384]{2,1,0:T(8,128)(2,1)S(1)}, u32[]{:S(2)}, u32[]{:S(2)}) collective-permute-start(bf16[32,16,384]{2,1,0:T(8,128)(2,1)S(1)} %collective-permute-done.6.refs_5_), channel_id=1, source_target_pairs={{0,2},{2,4},{4,6},{6,8},{8,10},{10,12},{12,14},{14,0},{1,3},{3,5},... | collective-permute-start | bytes 1179656 | tf_op jit(solution)/shard_map/ppermute | solution.py:176
  81.7 6.5 %collective-permute-done.3.refs_3_ = bf16[32,16,384]{2,1,0:T(8,128)(2,1)S(1)} collective-permute-done((bf16[32,16,384]{2,1,0:T(8,128)(2,1)S(1)}, bf16[32,16,384]{2,1,0:T(8,128)(2,1)S(1)}, u32[]{:S(2)}, u32[]{:S(2)}) %collective-permute-start.3) | collective-permute-done | bytes 393248 | tf_op jit(solution)/shard_map/ppermute | solution.py:178
  88.2 5.0 %collective-permute-done.7.refs_4_ = bf16[32,16,384]{2,1,0:T(8,128)(2,1)S(1)} collective-permute-done((bf16[32,16,384]{2,1,0:T(8,128)(2,1)S(1)}, bf16[32,16,384]{2,1,0:T(8,128)(2,1)S(1)}, u32[]{:S(2)}, u32[]{:S(2)}) %collective-permute-start.7) | collective-permute-done | bytes 393248 | tf_op jit(solution)/shard_map/ppermute | solution.py:176
  93.2 14.2 %gram.1 = (f32[32,104,384]{2,1,0:T(8,128)}, f32[32,104,384]{2,1,0:T(8,128)}, f32[16,8,128]{2,1,0:T(8,128)S(1)}) custom-call(bf16[32,208,128]{2,1,0:T(8,128)(2,1)S(1)} %pad_maximum_fusion.cols_ref, bf16[32,16,384]{2,1,0:T(8,128)(2,1)S(1)} %bitcast.13, bf16[32,16,384]{2,1,0:T(8,128)(2,1)S(1)} %collective-permute-done.1.refs_1_, ...), custom_call_target="tpu_custom_call" | custom-call | tf_op jit(solution)/shard_map/gram/pallas_call | solution.py:200
  107.4 1.9 %collective-permute-start.8 = (f32[32,104,384]{2,1,0:T(8,128)}, f32[32,104,384]{2,1,0:T(8,128)}, u32[]{:S(2)}, u32[]{:S(2)}) collective-permute-start(f32[32,104,384]{2,1,0:T(8,128)} %get-tuple-element.10), channel_id=1, source_target_pairs={{0,1},{1,0},{2,3},{3,2},{4,5},{5,4},{6,7},{7,6},{8,9},{9,8},{10,11... | collective-permute-start | bytes 15335432 | tf_op jit(solution)/shard_map/ppermute | solution.py:222
  109.3 11.3 %all_to_all.25 = f32[16,8,128]{2,1,0:T(8,128)S(1)} all-to-all(f32[16,8,128]{2,1,0:T(8,128)S(1)} %get-tuple-element.8), channel_id=1, replica_groups=mesh['x'=4,'z'=8,'y'=8,'core'=2] {'z','core'}, dimensions={0} | all-to-all | bytes 131072 | tf_op jit(solution)/shard_map/all_to_all | solution.py:221
  121.3 8.1 %all-to-all-start.3 = ((f32[32,8,128]{2,1,0:T(8,128)}), f32[32,8,128]{2,1,0:T(8,128)S(1)}, u32[]{:S(2)}, u32[]{:S(2)}) async-start(f32[32,8,128]{2,1,0:T(8,128)} %broadcast_in_dim.10), calls=%async_computation.3 | async-start | bytes 262144 | tf_op jit(solution)/shard_map/all_to_all | solution.py:224
  129.4 10.3 %all-to-all-done.3.part_ref = f32[32,8,128]{2,1,0:T(8,128)S(1)} async-done(((f32[32,8,128]{2,1,0:T(8,128)}), f32[32,8,128]{2,1,0:T(8,128)S(1)}, u32[]{:S(2)}, u32[]{:S(2)}) %all-to-all-start.3) | async-done | bytes 131104 | tf_op jit(solution)/shard_map/all_to_all | solution.py:224
  139.7 4.5 %combine.1 = f32[2,384,128]{2,1,0:T(8,128)S(1)} custom-call(s32[1]{0:T(128)} %bitcast.core_ref, f32[32,8,128]{2,1,0:T(8,128)S(1)} %all-to-all-done.3.part_ref, f32[32,104,384]{2,1,0:T(8,128)} %get-tuple-element.9.own_ref, f32[32,104,384]{2,1,0:T(8,128)} %collective-permute-done.8.came_ref), custom_call_target="tpu_custom_call" | custom-call | tf_op jit(solution)/shard_map/combine/pallas_call | solution.py:226
  144.2 17.0 %all_to_all.26.pieces_ref = f32[32,24,128]{2,1,0:T(8,128)S(1)} all-to-all(f32[32,24,128]{2,1,0:T(8,128)S(1)} %bitcast.10), channel_id=1, replica_groups=mesh['x'=4,'z'=8,'y'=8,'core'=2] {'x','z'}, dimensions={0} | all-to-all | bytes 786432 | tf_op jit(solution)/shard_map/all_to_all | solution.py:245
  (15 shorter events, 3.9 us)
Async XLA Ops:
  0.0 15.4 %copy-start.1 = (bf16[128,3328]{1,0:T(8,128)(2,1)S(1)}, bf16[128,3328]{1,0:T(8,128)(2,1)}, u32[]{:S(2)}) copy-start(bf16[128,3328]{1,0:T(8,128)(2,1)} %param.4) | copy-start | bytes 2555908
  1.6 28.3 %all-to-all-start.1 = ((bf16[64,8,384]{2,1,0:T(8,128)(2,1)}), bf16[64,8,384]{2,1,0:T(8,128)(2,1)S(1)}, u32[]{:S(2)}, u32[]{:S(2)}) async-start(bf16[64,8,384]{2,1,0:T(8,128)(2,1)} %bitcast.5), calls=%async_computation.1 | async-start | bytes 786432 | tf_op jit(solution)/shard_map/all_to_all | solution.py:190
  29.9 30.5 %all-to-all-start = ((bf16[32,104,128]{2,1,0:T(8,128)(2,1)}), bf16[32,104,128]{2,1,0:T(8,128)(2,1)S(1)}, u32[]{:S(2)}, u32[]{:S(2)}) async-start(bf16[32,104,128]{2,1,0:T(8,128)(2,1)} %bitcast.2), calls=%async_computation | async-start | bytes 1703936 | tf_op jit(solution)/shard_map/all_to_all | solution.py:196
  35.5 12.5 %collective-permute-start.4 = (bf16[32,16,384]{2,1,0:T(8,128)(2,1)S(1)}, bf16[32,16,384]{2,1,0:T(8,128)(2,1)S(1)}, u32[]{:S(2)}, u32[]{:S(2)}) collective-permute-start(bf16[32,16,384]{2,1,0:T(8,128)(2,1)S(1)} %bitcast.11), channel_id=1, source_target_pairs={{0,2},{2,4},{4,6},{6,8},{8,10},{10,12},{12,14},{14,0},{1,3},{3,5},... | collective-permute-start | bytes 1179656 | tf_op jit(solution)/shard_map/ppermute | solution.py:176
  39.0 23.2 %collective-permute-start.1 = (bf16[32,16,384]{2,1,0:T(8,128)(2,1)S(1)}, bf16[32,16,384]{2,1,0:T(8,128)(2,1)S(1)}, u32[]{:S(2)}, u32[]{:S(2)}) collective-permute-start(bf16[32,16,384]{2,1,0:T(8,128)(2,1)S(1)} %bitcast.12), channel_id=1, source_target_pairs={{0,14},{2,0},{4,2},{6,4},{8,6},{10,8},{12,10},{14,12},{1,15},{3,1}... | collective-permute-start | bytes 1179656 | tf_op jit(solution)/shard_map/ppermute | solution.py:178
  48.1 16.5 %collective-permute-start.5 = (bf16[32,16,384]{2,1,0:T(8,128)(2,1)S(1)}, bf16[32,16,384]{2,1,0:T(8,128)(2,1)S(1)}, u32[]{:S(2)}, u32[]{:S(2)}) collective-permute-start(bf16[32,16,384]{2,1,0:T(8,128)(2,1)S(1)} %collective-permute-done.4.refs_7_), channel_id=1, source_target_pairs={{0,2},{2,4},{4,6},{6,8},{8,10},{10,12},{12,14},{14,0},{1,3},{3,5},... | collective-permute-start | bytes 1179656 | tf_op jit(solution)/shard_map/ppermute | solution.py:176
  60.3 21.2 %collective-permute-start = (bf16[32,104,128]{2,1,0:T(8,128)(2,1)S(1)}, bf16[32,104,128]{2,1,0:T(8,128)(2,1)S(1)}, u32[]{:S(2)}, u32[]{:S(2)}) collective-permute-start(bf16[32,104,128]{2,1,0:T(8,128)(2,1)S(1)} %all-to-all-done), channel_id=1, source_target_pairs={{0,1},{1,0},{2,3},{3,2},{4,5},{5,4},{6,7},{7,6},{8,9},{9,8},{10,11... | collective-permute-start | bytes 2555912 | tf_op jit(solution)/shard_map/ppermute | solution.py:197
  62.2 13.4 %collective-permute-start.2 = (bf16[32,16,384]{2,1,0:T(8,128)(2,1)S(1)}, bf16[32,16,384]{2,1,0:T(8,128)(2,1)S(1)}, u32[]{:S(2)}, u32[]{:S(2)}) collective-permute-start(bf16[32,16,384]{2,1,0:T(8,128)(2,1)S(1)} %collective-permute-done.1.refs_1_), channel_id=1, source_target_pairs={{0,14},{2,0},{4,2},{6,4},{8,6},{10,8},{12,10},{14,12},{1,15},{3,1}... | collective-permute-start | bytes 1179656 | tf_op jit(solution)/shard_map/ppermute | solution.py:178
  64.6 14.9 %collective-permute-start.6 = (bf16[32,16,384]{2,1,0:T(8,128)(2,1)S(1)}, bf16[32,16,384]{2,1,0:T(8,128)(2,1)S(1)}, u32[]{:S(2)}, u32[]{:S(2)}) collective-permute-start(bf16[32,16,384]{2,1,0:T(8,128)(2,1)S(1)} %collective-permute-done.5.refs_6_), channel_id=1, source_target_pairs={{0,2},{2,4},{4,6},{6,8},{8,10},{10,12},{12,14},{14,0},{1,3},{3,5},... | collective-permute-start | bytes 1179656 | tf_op jit(solution)/shard_map/ppermute | solution.py:176
  75.7 12.5 %collective-permute-start.3 = (bf16[32,16,384]{2,1,0:T(8,128)(2,1)S(1)}, bf16[32,16,384]{2,1,0:T(8,128)(2,1)S(1)}, u32[]{:S(2)}, u32[]{:S(2)}) collective-permute-start(bf16[32,16,384]{2,1,0:T(8,128)(2,1)S(1)} %collective-permute-done.2.refs_2_), channel_id=1, source_target_pairs={{0,14},{2,0},{4,2},{6,4},{8,6},{10,8},{12,10},{14,12},{1,15},{3,1}... | collective-permute-start | bytes 1179656 | tf_op jit(solution)/shard_map/ppermute | solution.py:178
  79.5 13.8 %collective-permute-start.7 = (bf16[32,16,384]{2,1,0:T(8,128)(2,1)S(1)}, bf16[32,16,384]{2,1,0:T(8,128)(2,1)S(1)}, u32[]{:S(2)}, u32[]{:S(2)}) collective-permute-start(bf16[32,16,384]{2,1,0:T(8,128)(2,1)S(1)} %collective-permute-done.6.refs_5_), channel_id=1, source_target_pairs={{0,2},{2,4},{4,6},{6,8},{8,10},{10,12},{12,14},{14,0},{1,3},{3,5},... | collective-permute-start | bytes 1179656 | tf_op jit(solution)/shard_map/ppermute | solution.py:176
  107.4 32.3 %collective-permute-start.8 = (f32[32,104,384]{2,1,0:T(8,128)}, f32[32,104,384]{2,1,0:T(8,128)}, u32[]{:S(2)}, u32[]{:S(2)}) collective-permute-start(f32[32,104,384]{2,1,0:T(8,128)} %get-tuple-element.10), channel_id=1, source_target_pairs={{0,1},{1,0},{2,3},{3,2},{4,5},{5,4},{6,7},{7,6},{8,9},{9,8},{10,11... | collective-permute-start | bytes 15335432 | tf_op jit(solution)/shard_map/ppermute | solution.py:222
  121.3 18.4 %all-to-all-start.3 = ((f32[32,8,128]{2,1,0:T(8,128)}), f32[32,8,128]{2,1,0:T(8,128)S(1)}, u32[]{:S(2)}, u32[]{:S(2)}) async-start(f32[32,8,128]{2,1,0:T(8,128)} %broadcast_in_dim.10), calls=%async_computation.3 | async-start | bytes 262144 | tf_op jit(solution)/shard_map/all_to_all | solution.py:224
  139.7 21.5 %copy-start = (f32[24,3328]{1,0:T(8,128)S(1)}, f32[24,3328]{1,0:T(8,128)}, u32[]{:S(2)}) copy-start(f32[24,3328]{1,0:T(8,128)} %momentum_ref.1) | copy-start | bytes 958468

commit v3 on v2

--- a/solution.py
+++ b/solution.py
@@ -1,3 +1,5 @@
+import functools
+
 import jax
 import jax.numpy as jnp
 from jax import lax
@@ -9,31 +11,38 @@
 EPSILON = 1e-06
 DECAY = 0.9
 NR = 32
+GRANTS = (48, 48)
 TOK = 128
 LANES = 128
 XZ = ("x", "z")
 CORES = [(0, 1), (1, 0)]
+CHUNKS = ((0, 128), (128, 256))
 PIECES = ((0, 56), (56, 48))
 
 
-def gram_kernel(cols_ref, *refs):
+def gram_kernel(start, n_before, cols_ref, *refs):
+    before, refs = refs[2 * n_before : n_before * 3], refs[3 * n_before :]
     act_refs, outs, (gram_ref, g_ref, q_ref, sem) = refs[:-6], refs[-6:-4], refs[-4:]
     groups = cols_ref.shape[1] // 8
-    depth = act_refs[0].shape[-1]
+    depth = g_ref.shape[-1]
     lane_blocks = depth // LANES
     unroll = 26
     assert groups % unroll == 0
-
-    def one(r, carry):
-        act = jnp.concatenate([ref[r] for ref in act_refs], axis=0)
+    opposite = len(act_refs) // 2
+
+    for r in range(NR):
+        rows = [
+            ref[r] if k == opposite else ref[r, :, start : start + depth]
+            for k, ref in enumerate(act_refs)
+        ]
+        act = jnp.concatenate(rows, axis=0)
         g_ref[r] = jnp.dot(cols_ref[r], act, preferred_element_type=jnp.float32)
-        return carry
-
-    lax.fori_loop(0, NR, one, 0, unroll=NR)
+
     saves = []
     for part, out in enumerate(outs):
         rows = pl.ds(part * out.shape[1], out.shape[1])
-        saves.append(pltpu.make_async_copy(g_ref.at[:, rows], out, sem.at[part]))
+        place = out.at[:, :, pl.ds(start, depth)]
+        saves.append(pltpu.make_async_copy(g_ref.at[:, rows], place, sem.at[part]))
         saves[-1].start()
     q_ref[...] = jnp.zeros_like(q_ref)
 
@@ -80,6 +89,8 @@
     )
     for i in range(8):
         row = sums[i : i + 1, i * LANES : (i + 1) * LANES]
+        for ref in before:
+            row = row + ref[0, i : i + 1, :]
         for k in range(gram_ref.shape[0]):
             gram_ref[k, i : i + 1, :] = row
     for save in saves:
@@ -172,11 +183,14 @@
     up = [(i, (i + 1) % size) for i in range(size)]
     down = [(i, (i - 1) % size) for i in range(size)]
     above, below = [block], [block]
-    for step in range(size // 2):
+    for _ in range(size // 2 - 1):
         below.append(lax.ppermute(below[-1], "y", up))
-        if step < size // 2 - 1:
-            above.append(lax.ppermute(above[-1], "y", down))
-    return above + below[:0:-1]
+        above.append(lax.ppermute(above[-1], "y", down))
+    opposite = []
+    for start, width in CHUNKS:
+        part = below[-1][:, :, start : start + width]
+        opposite.append(lax.ppermute(part, "y", up))
+    return above, opposite, below[:0:-1]
 
 
 def local(activations, grad_out, momentum):
@@ -192,31 +206,38 @@
 
     shift = 16 * lax.axis_index("y")
     rolled = lax.dynamic_slice_in_dim(jnp.concatenate([grad_out, grad_out], axis=0), shift, TOK, 0)
-    acts = ring(halves.reshape(NR, 16, depth))
+    above, opposite, below = ring(halves.reshape(NR, 16, depth))
     own = lax.all_to_all(rolled.T.reshape(NR, share, TOK), XZ, 0, 0, tiled=True)
     other = lax.ppermute(own, "core", CORES)
     cols = jnp.concatenate([own, other], axis=1)
 
-    grads, to_swap, gram = pl.pallas_call(
-        gram_kernel,
-        out_shape=[
-            jax.ShapeDtypeStruct((NR, share, depth), jnp.float32),
-            jax.ShapeDtypeStruct((NR, share, depth), jnp.float32),
-            jax.ShapeDtypeStruct((16, 8, LANES), jnp.float32),
-        ],
-        out_specs=[
-            pl.BlockSpec(memory_space=pltpu.HBM),
-            pl.BlockSpec(memory_space=pltpu.HBM),
-            pl.BlockSpec(memory_space=pltpu.VMEM),
-        ],
-        scratch_shapes=[
-            pltpu.VMEM((NR, 2 * share, depth), jnp.float32),
-            pltpu.VMEM((1024, LANES), jnp.float32),
-            pltpu.SemaphoreType.DMA((2,)),
-        ],
-        compiler_params=pltpu.CompilerParams(vmem_limit_bytes=48 << 20),
-        name="gram",
-    )(cols, *acts)
+    carried = ()
+    for k, (start, width) in enumerate(CHUNKS):
+        carried = pl.pallas_call(
+            functools.partial(gram_kernel, start, k),
+            out_shape=[
+                jax.ShapeDtypeStruct((NR, share, depth), jnp.float32),
+                jax.ShapeDtypeStruct((NR, share, depth), jnp.float32),
+                jax.ShapeDtypeStruct((16, 8, LANES), jnp.float32),
+            ],
+            in_specs=[pl.BlockSpec(memory_space=pltpu.VMEM)]
+            + [pl.BlockSpec(memory_space=pltpu.HBM)] * (2 * k)
+            + [pl.BlockSpec(memory_space=pltpu.VMEM)] * (8 + k),
+            out_specs=[
+                pl.BlockSpec(memory_space=pltpu.HBM),
+                pl.BlockSpec(memory_space=pltpu.HBM),
+                pl.BlockSpec(memory_space=pltpu.VMEM),
+            ],
+            scratch_shapes=[
+                pltpu.VMEM((NR, 2 * share, width), jnp.float32),
+                pltpu.VMEM((1024, LANES), jnp.float32),
+                pltpu.SemaphoreType.DMA((2,)),
+            ],
+            input_output_aliases={1: 0, 2: 1} if k else {},
+            compiler_params=pltpu.CompilerParams(vmem_limit_bytes=GRANTS[k] << 20),
+            name="gram",
+        )(cols, *carried, *above, opposite[k], *below)
+    grads, to_swap, gram = carried
 
     gram = lax.all_to_all(gram, ("z", "core"), 0, 0, tiled=True)
     came = lax.ppermute(to_swap, "core", CORES)

time: 163 us -> 164 us (level)
  starting transfers between devices: 51.9 us -> 56.2 us
  waiting for transfers between devices: 58.1 us -> 53.8 us
    ppermute x0 -> x2, starting transfers between devices: none -> 6.28 us  [ring(): opposite.append(lax.ppermute(part, 'y', up))]
    ppermute x0 -> x2, waiting for transfers between devices: none -> 5.07 us  [ring(): opposite.append(lax.ppermute(part, 'y', up))]
    ppermute x4 -> x3, waiting for transfers between devices: 12.2 us -> 7.18 us  [ring(): below.append(lax.ppermute(below[-1], 'y', up))]
    ppermute x3, waiting for transfers between devices: 14.1 us -> 9.69 us  [ring(): above.append(lax.ppermute(above[-1], 'y', down))]
    ppermute x4 -> x3, starting transfers between devices: 12.5 us -> 10.4 us  [ring(): below.append(lax.ppermute(below[-1], 'y', up))]
    pallas_call x1 -> x2, Pallas kernels: 14.2 us -> 15.5 us  [local(): pl.pallas_call(functools.partial(gram_kernel, start, k), out_shape=[jax.S...]
  transfers between devices with their start and end apart: 12 -> 13, of which waited for: 8 -> 8; matrix products, arithmetic and copies ran while one was open for 2% -> 2% of each run, Pallas kernels for 0% -> 4%
where the time goes in v3:
time: 164 us; the launch traced here: 163 us
  starting transfers between devices  56.2 us (34%)
  waiting for transfers between devices  53.8 us (33%)
  blocking collectives  28.3 us (17%)
  Pallas kernels  20.8 us (13%)
  local copies, waits for them, and re-layouts  3.74 us (2%)
    all_to_all x1, blocking collectives, local(): pieces = lax.all_to_all(pieces, XZ, 0, 0, tiled=True)  17 us
    pallas_call x2, Pallas kernels, local(): pl.pallas_call(functools.partial(gram_kernel, start, k), out_shape=[jax.S...  15.5 us
    all_to_all x1, starting transfers between devices, local(): halves = lax.all_to_all(halves, ('x', 'z', 'core'), 0, 0, tiled=True)  13.8 us
    all_to_all x1, waiting for transfers between devices, local(): halves = lax.all_to_all(halves, ('x', 'z', 'core'), 0, 0, tiled=True)  12.8 us
    all_to_all x1, blocking collectives, local(): gram = lax.all_to_all(gram, ('z', 'core'), 0, 0, tiled=True)  11.3 us
    ppermute x3, starting transfers between devices, ring(): below.append(lax.ppermute(below[-1], 'y', up))  10.4 us
    all_to_all x1, waiting for transfers between devices, local(): lax.all_to_all(jnp.broadcast_to(gram, (32, 8, LANES)), ('x', 'y'), 0, 0,...  10.3 us
    ppermute x3, waiting for transfers between devices, ring(): above.append(lax.ppermute(above[-1], 'y', down))  9.69 us
  transfers between devices with their start and end apart: 13, of which 8 were waited for; matrix products, arithmetic and copies ran while one was open for 2% of the time, Pallas kernels for 4%

profile of v3, /device:TPU:8, one launch (start us, length us, event | category | flops | bytes accessed | tf_op | source)
XLA Modules:
  0.0 163.5 jit_solution(11970042087415423543)
XLA Ops:
  1.6 13.8 %all-to-all-start.1 = ((bf16[64,8,384]{2,1,0:T(8,128)(2,1)}), bf16[64,8,384]{2,1,0:T(8,128)(2,1)S(1)}, u32[]{:S(2)}, u32[]{:S(2)}) async-start(bf16[64,8,384]{2,1,0:T(8,128)(2,1)} %bitcast.5), calls=%async_computation.1 | async-start | bytes 786432 | tf_op jit(solution)/shard_map/all_to_all | solution.py:204
  17.1 12.8 %all-to-all-done.1 = bf16[64,8,384]{2,1,0:T(8,128)(2,1)S(1)} async-done(((bf16[64,8,384]{2,1,0:T(8,128)(2,1)}), bf16[64,8,384]{2,1,0:T(8,128)(2,1)S(1)}, u32[]{:S(2)}, u32[]{:S(2)}) %all-to-all-start.1) | async-done | bytes 393248 | tf_op jit(solution)/shard_map/all_to_all | solution.py:204
  29.9 5.7 %all-to-all-start = ((bf16[32,104,128]{2,1,0:T(8,128)(2,1)}), bf16[32,104,128]{2,1,0:T(8,128)(2,1)S(1)}, u32[]{:S(2)}, u32[]{:S(2)}) async-start(bf16[32,104,128]{2,1,0:T(8,128)(2,1)} %bitcast.2), calls=%async_computation | async-start | bytes 1703936 | tf_op jit(solution)/shard_map/all_to_all | solution.py:210
  35.6 3.5 %collective-permute-start.4 = (bf16[32,16,384]{2,1,0:T(8,128)(2,1)S(1)}, bf16[32,16,384]{2,1,0:T(8,128)(2,1)S(1)}, u32[]{:S(2)}, u32[]{:S(2)}) collective-permute-start(bf16[32,16,384]{2,1,0:T(8,128)(2,1)S(1)} %bitcast.10), channel_id=1, source_target_pairs={{0,2},{2,4},{4,6},{6,8},{8,10},{10,12},{12,14},{14,0},{1,3},{3,5},... | collective-permute-start | bytes 1179656 | tf_op jit(solution)/shard_map/ppermute | solution.py:187
  39.0 2.4 %collective-permute-start.1 = (bf16[32,16,384]{2,1,0:T(8,128)(2,1)S(1)}, bf16[32,16,384]{2,1,0:T(8,128)(2,1)S(1)}, u32[]{:S(2)}, u32[]{:S(2)}) collective-permute-start(bf16[32,16,384]{2,1,0:T(8,128)(2,1)S(1)} %bitcast.11), channel_id=1, source_target_pairs={{0,14},{2,0},{4,2},{6,4},{8,6},{10,8},{12,10},{14,12},{1,15},{3,1}... | collective-permute-start | bytes 1179656 | tf_op jit(solution)/shard_map/ppermute | solution.py:188
  41.4 6.7 %collective-permute-done.4.refs_7_.refs_10_ = bf16[32,16,384]{2,1,0:T(8,128)(2,1)S(1)} collective-permute-done((bf16[32,16,384]{2,1,0:T(8,128)(2,1)S(1)}, bf16[32,16,384]{2,1,0:T(8,128)(2,1)S(1)}, u32[]{:S(2)}, u32[]{:S(2)}) %collective-permute-start.4) | collective-permute-done | bytes 393248 | tf_op jit(solution)/shard_map/ppermute | solution.py:187
  48.1 3.5 %collective-permute-start.5 = (bf16[32,16,384]{2,1,0:T(8,128)(2,1)S(1)}, bf16[32,16,384]{2,1,0:T(8,128)(2,1)S(1)}, u32[]{:S(2)}, u32[]{:S(2)}) collective-permute-start(bf16[32,16,384]{2,1,0:T(8,128)(2,1)S(1)} %collective-permute-done.4.refs_7_.refs_10_), channel_id=1, source_target_pairs={{0,2},{2,4},{4,6},{6,8},{8,10},{10,12},{12,14},{14,0},{1,3},{3,5},... | collective-permute-start | bytes 1179656 | tf_op jit(solution)/shard_map/ppermute | solution.py:187
  51.6 8.7 %all-to-all-done = bf16[32,104,128]{2,1,0:T(8,128)(2,1)S(1)} async-done(((bf16[32,104,128]{2,1,0:T(8,128)(2,1)}), bf16[32,104,128]{2,1,0:T(8,128)(2,1)S(1)}, u32[]{:S(2)}, u32[]{:S(2)}) %all-to-all-start) | async-done | bytes 852000 | tf_op jit(solution)/shard_map/all_to_all | solution.py:210
  62.3 2.4 %collective-permute-start.2 = (bf16[32,16,384]{2,1,0:T(8,128)(2,1)S(1)}, bf16[32,16,384]{2,1,0:T(8,128)(2,1)S(1)}, u32[]{:S(2)}, u32[]{:S(2)}) collective-permute-start(bf16[32,16,384]{2,1,0:T(8,128)(2,1)S(1)} %collective-permute-done.1.refs_1_.refs_4_), channel_id=1, source_target_pairs={{0,14},{2,0},{4,2},{6,4},{8,6},{10,8},{12,10},{14,12},{1,15},{3,1}... | collective-permute-start | bytes 1179656 | tf_op jit(solution)/shard_map/ppermute | solution.py:188
  64.6 3.5 %collective-permute-start.6 = (bf16[32,16,384]{2,1,0:T(8,128)(2,1)S(1)}, bf16[32,16,384]{2,1,0:T(8,128)(2,1)S(1)}, u32[]{:S(2)}, u32[]{:S(2)}) collective-permute-start(bf16[32,16,384]{2,1,0:T(8,128)(2,1)S(1)} %collective-permute-done.5.refs_6_.refs_9_), channel_id=1, source_target_pairs={{0,2},{2,4},{4,6},{6,8},{8,10},{10,12},{12,14},{14,0},{1,3},{3,5},... | collective-permute-start | bytes 1179656 | tf_op jit(solution)/shard_map/ppermute | solution.py:187
  68.1 7.5 %collective-permute-done.2.refs_2_.refs_5_ = bf16[32,16,384]{2,1,0:T(8,128)(2,1)S(1)} collective-permute-done((bf16[32,16,384]{2,1,0:T(8,128)(2,1)S(1)}, bf16[32,16,384]{2,1,0:T(8,128)(2,1)S(1)}, u32[]{:S(2)}, u32[]{:S(2)}) %collective-permute-start.2) | collective-permute-done | bytes 393248 | tf_op jit(solution)/shard_map/ppermute | solution.py:188
  75.7 3.3 %collective-permute-start.3 = (bf16[32,16,384]{2,1,0:T(8,128)(2,1)S(1)}, bf16[32,16,384]{2,1,0:T(8,128)(2,1)S(1)}, u32[]{:S(2)}, u32[]{:S(2)}) collective-permute-start(bf16[32,16,384]{2,1,0:T(8,128)(2,1)S(1)} %collective-permute-done.2.refs_2_.refs_5_), channel_id=1, source_target_pairs={{0,14},{2,0},{4,2},{6,4},{8,6},{10,8},{12,10},{14,12},{1,15},{3,1}... | collective-permute-start | bytes 1179656 | tf_op jit(solution)/shard_map/ppermute | solution.py:188
  79.5 2.0 %collective-permute-start.8 = (bf16[32,16,256]{2,1,0:T(8,128)(2,1)S(1)}, bf16[32,16,256]{2,1,0:T(8,128)(2,1)S(1)}, u32[]{:S(2)}, u32[]{:S(2)}) collective-permute-start(bf16[32,16,256]{2,1,0:T(8,128)(2,1)S(1)} %slice.9), channel_id=1, source_target_pairs={{0,2},{2,4},{4,6},{6,8},{8,10},{10,12},{12,14},{14,0},{1,3},{3,5},... | collective-permute-start | bytes 786440 | tf_op jit(solution)/shard_map/ppermute | solution.py:192
  81.7 4.3 %collective-permute-start.7 = (bf16[32,16,128]{2,1,0:T(8,128)(2,1)S(1)}, bf16[32,16,128]{2,1,0:T(8,128)(2,1)S(1)}, u32[]{:S(2)}, u32[]{:S(2)}) collective-permute-start(bf16[32,16,128]{2,1,0:T(8,128)(2,1)S(1)} %slice.8), channel_id=1, source_target_pairs={{0,2},{2,4},{4,6},{6,8},{8,10},{10,12},{12,14},{14,0},{1,3},{3,5},... | collective-permute-start | bytes 393224 | tf_op jit(solution)/shard_map/ppermute | solution.py:192
  86.1 2.1 %collective-permute-done.3.refs_3_.refs_6_ = bf16[32,16,384]{2,1,0:T(8,128)(2,1)S(1)} collective-permute-done((bf16[32,16,384]{2,1,0:T(8,128)(2,1)S(1)}, bf16[32,16,384]{2,1,0:T(8,128)(2,1)S(1)}, u32[]{:S(2)}, u32[]{:S(2)}) %collective-permute-start.3) | collective-permute-done | bytes 393248 | tf_op jit(solution)/shard_map/ppermute | solution.py:188
  88.2 5.1 %collective-permute-done.7.refs_4_ = bf16[32,16,128]{2,1,0:T(8,128)(2,1)S(1)} collective-permute-done((bf16[32,16,128]{2,1,0:T(8,128)(2,1)S(1)}, bf16[32,16,128]{2,1,0:T(8,128)(2,1)S(1)}, u32[]{:S(2)}, u32[]{:S(2)}) %collective-permute-start.7) | collective-permute-done | bytes 131104 | tf_op jit(solution)/shard_map/ppermute | solution.py:192
  93.3 5.9 %gram.2 = (f32[32,104,384]{2,1,0:T(8,128)}, f32[32,104,384]{2,1,0:T(8,128)}, f32[16,8,128]{2,1,0:T(8,128)S(1)}) custom-call(bf16[32,208,128]{2,1,0:T(8,128)(2,1)S(1)} %constant_dynamic-update-slice_fusion.cols_ref, bf16[32,16,384]{2,1,0:T(8,128)(2,1)S(1)} %bitcast.12, bf16[32,16,384]{2,1,0:T(8,128)(2,1)S(1)} %collective-permute-done.1.refs_1_.refs_4_, ...), custom_call_target="tpu_custom_call" | custom-call | tf_op jit(solution)/shard_map/gram/pallas_call | solution.py:216
  99.2 9.6 %gram.3 = (f32[32,104,384]{2,1,0:T(8,128)}, f32[32,104,384]{2,1,0:T(8,128)}, f32[16,8,128]{2,1,0:T(8,128)S(1)}) custom-call(bf16[32,208,128]{2,1,0:T(8,128)(2,1)S(1)} %constant_dynamic-update-slice_fusion.cols_ref, f32[32,104,384]{2,1,0:T(8,128)} %get-tuple-element.11.refs_0_, ...), custom_call_target="tpu_custom_call", output_to_operand_aliasing={{0}: (1, {}), {1}: (2, {})} | custom-call | tf_op jit(solution)/shard_map/gram/pallas_call | solution.py:216
  108.8 1.9 %collective-permute-start.9 = (f32[32,104,384]{2,1,0:T(8,128)}, f32[32,104,384]{2,1,0:T(8,128)}, u32[]{:S(2)}, u32[]{:S(2)}) collective-permute-start(f32[32,104,384]{2,1,0:T(8,128)} %get-tuple-element.16), channel_id=1, source_target_pairs={{0,1},{1,0},{2,3},{3,2},{4,5},{5,4},{6,7},{7,6},{8,9},{9,8},{10,11... | collective-permute-start | bytes 15335432 | tf_op jit(solution)/shard_map/ppermute | solution.py:243
  110.7 11.3 %all_to_all.25 = f32[16,8,128]{2,1,0:T(8,128)S(1)} all-to-all(f32[16,8,128]{2,1,0:T(8,128)S(1)} %get-tuple-element.14), channel_id=1, replica_groups=mesh['x'=4,'z'=8,'y'=8,'core'=2] {'z','core'}, dimensions={0} | all-to-all | bytes 131072 | tf_op jit(solution)/shard_map/all_to_all | solution.py:242
  122.7 8.1 %all-to-all-start.3 = ((f32[32,8,128]{2,1,0:T(8,128)}), f32[32,8,128]{2,1,0:T(8,128)S(1)}, u32[]{:S(2)}, u32[]{:S(2)}) async-start(f32[32,8,128]{2,1,0:T(8,128)} %broadcast_in_dim.10), calls=%async_computation.3 | async-start | bytes 262144 | tf_op jit(solution)/shard_map/all_to_all | solution.py:245
  130.8 10.3 %all-to-all-done.3.part_ref = f32[32,8,128]{2,1,0:T(8,128)S(1)} async-done(((f32[32,8,128]{2,1,0:T(8,128)}), f32[32,8,128]{2,1,0:T(8,128)S(1)}, u32[]{:S(2)}, u32[]{:S(2)}) %all-to-all-start.3) | async-done | bytes 131104 | tf_op jit(solution)/shard_map/all_to_all | solution.py:245
  141.1 4.5 %combine.1 = f32[2,384,128]{2,1,0:T(8,128)S(1)} custom-call(s32[1]{0:T(128)} %bitcast.core_ref, f32[32,8,128]{2,1,0:T(8,128)S(1)} %all-to-all-done.3.part_ref, f32[32,104,384]{2,1,0:T(8,128)} %get-tuple-element.15.own_ref, f32[32,104,384]{2,1,0:T(8,128)} %collective-permute-done.9.came_ref), custom_call_target="tpu_custom_call" | custom-call | tf_op jit(solution)/shard_map/combine/pallas_call | solution.py:247
  145.6 17.0 %all_to_all.26.pieces_ref = f32[32,24,128]{2,1,0:T(8,128)S(1)} all-to-all(f32[32,24,128]{2,1,0:T(8,128)S(1)} %bitcast.14), channel_id=1, replica_groups=mesh['x'=4,'z'=8,'y'=8,'core'=2] {'x','z'}, dimensions={0} | all-to-all | bytes 786432 | tf_op jit(solution)/shard_map/all_to_all | solution.py:266
  (21 shorter events, 7.5 us)
Async XLA Ops:
  0.0 15.4 %copy-start.1 = (bf16[128,3328]{1,0:T(8,128)(2,1)S(1)}, bf16[128,3328]{1,0:T(8,128)(2,1)}, u32[]{:S(2)}) copy-start(bf16[128,3328]{1,0:T(8,128)(2,1)} %param.4) | copy-start | bytes 2555908
  1.6 28.3 %all-to-all-start.1 = ((bf16[64,8,384]{2,1,0:T(8,128)(2,1)}), bf16[64,8,384]{2,1,0:T(8,128)(2,1)S(1)}, u32[]{:S(2)}, u32[]{:S(2)}) async-start(bf16[64,8,384]{2,1,0:T(8,128)(2,1)} %bitcast.5), calls=%async_computation.1 | async-start | bytes 786432 | tf_op jit(solution)/shard_map/all_to_all | solution.py:204
  29.9 30.5 %all-to-all-start = ((bf16[32,104,128]{2,1,0:T(8,128)(2,1)}), bf16[32,104,128]{2,1,0:T(8,128)(2,1)S(1)}, u32[]{:S(2)}, u32[]{:S(2)}) async-start(bf16[32,104,128]{2,1,0:T(8,128)(2,1)} %bitcast.2), calls=%async_computation | async-start | bytes 1703936 | tf_op jit(solution)/shard_map/all_to_all | solution.py:210
  35.6 12.5 %collective-permute-start.4 = (bf16[32,16,384]{2,1,0:T(8,128)(2,1)S(1)}, bf16[32,16,384]{2,1,0:T(8,128)(2,1)S(1)}, u32[]{:S(2)}, u32[]{:S(2)}) collective-permute-start(bf16[32,16,384]{2,1,0:T(8,128)(2,1)S(1)} %bitcast.10), channel_id=1, source_target_pairs={{0,2},{2,4},{4,6},{6,8},{8,10},{10,12},{12,14},{14,0},{1,3},{3,5},... | collective-permute-start | bytes 1179656 | tf_op jit(solution)/shard_map/ppermute | solution.py:187
  39.0 23.2 %collective-permute-start.1 = (bf16[32,16,384]{2,1,0:T(8,128)(2,1)S(1)}, bf16[32,16,384]{2,1,0:T(8,128)(2,1)S(1)}, u32[]{:S(2)}, u32[]{:S(2)}) collective-permute-start(bf16[32,16,384]{2,1,0:T(8,128)(2,1)S(1)} %bitcast.11), channel_id=1, source_target_pairs={{0,14},{2,0},{4,2},{6,4},{8,6},{10,8},{12,10},{14,12},{1,15},{3,1}... | collective-permute-start | bytes 1179656 | tf_op jit(solution)/shard_map/ppermute | solution.py:188
  48.1 16.5 %collective-permute-start.5 = (bf16[32,16,384]{2,1,0:T(8,128)(2,1)S(1)}, bf16[32,16,384]{2,1,0:T(8,128)(2,1)S(1)}, u32[]{:S(2)}, u32[]{:S(2)}) collective-permute-start(bf16[32,16,384]{2,1,0:T(8,128)(2,1)S(1)} %collective-permute-done.4.refs_7_.refs_10_), channel_id=1, source_target_pairs={{0,2},{2,4},{4,6},{6,8},{8,10},{10,12},{12,14},{14,0},{1,3},{3,5},... | collective-permute-start | bytes 1179656 | tf_op jit(solution)/shard_map/ppermute | solution.py:187
  60.3 25.6 %collective-permute-start = (bf16[32,104,128]{2,1,0:T(8,128)(2,1)S(1)}, bf16[32,104,128]{2,1,0:T(8,128)(2,1)S(1)}, u32[]{:S(2)}, u32[]{:S(2)}) collective-permute-start(bf16[32,104,128]{2,1,0:T(8,128)(2,1)S(1)} %all-to-all-done), channel_id=1, source_target_pairs={{0,1},{1,0},{2,3},{3,2},{4,5},{5,4},{6,7},{7,6},{8,9},{9,8},{10,11... | collective-permute-start | bytes 2555912 | tf_op jit(solution)/shard_map/ppermute | solution.py:211
  62.3 13.4 %collective-permute-start.2 = (bf16[32,16,384]{2,1,0:T(8,128)(2,1)S(1)}, bf16[32,16,384]{2,1,0:T(8,128)(2,1)S(1)}, u32[]{:S(2)}, u32[]{:S(2)}) collective-permute-start(bf16[32,16,384]{2,1,0:T(8,128)(2,1)S(1)} %collective-permute-done.1.refs_1_.refs_4_), channel_id=1, source_target_pairs={{0,14},{2,0},{4,2},{6,4},{8,6},{10,8},{12,10},{14,12},{1,15},{3,1}... | collective-permute-start | bytes 1179656 | tf_op jit(solution)/shard_map/ppermute | solution.py:188
  64.6 14.9 %collective-permute-start.6 = (bf16[32,16,384]{2,1,0:T(8,128)(2,1)S(1)}, bf16[32,16,384]{2,1,0:T(8,128)(2,1)S(1)}, u32[]{:S(2)}, u32[]{:S(2)}) collective-permute-start(bf16[32,16,384]{2,1,0:T(8,128)(2,1)S(1)} %collective-permute-done.5.refs_6_.refs_9_), channel_id=1, source_target_pairs={{0,2},{2,4},{4,6},{6,8},{8,10},{10,12},{12,14},{14,0},{1,3},{3,5},... | collective-permute-start | bytes 1179656 | tf_op jit(solution)/shard_map/ppermute | solution.py:187
  75.7 12.5 %collective-permute-start.3 = (bf16[32,16,384]{2,1,0:T(8,128)(2,1)S(1)}, bf16[32,16,384]{2,1,0:T(8,128)(2,1)S(1)}, u32[]{:S(2)}, u32[]{:S(2)}) collective-permute-start(bf16[32,16,384]{2,1,0:T(8,128)(2,1)S(1)} %collective-permute-done.2.refs_2_.refs_5_), channel_id=1, source_target_pairs={{0,14},{2,0},{4,2},{6,4},{8,6},{10,8},{12,10},{14,12},{1,15},{3,1}... | collective-permute-start | bytes 1179656 | tf_op jit(solution)/shard_map/ppermute | solution.py:188
  79.5 19.6 %collective-permute-start.8 = (bf16[32,16,256]{2,1,0:T(8,128)(2,1)S(1)}, bf16[32,16,256]{2,1,0:T(8,128)(2,1)S(1)}, u32[]{:S(2)}, u32[]{:S(2)}) collective-permute-start(bf16[32,16,256]{2,1,0:T(8,128)(2,1)S(1)} %slice.9), channel_id=1, source_target_pairs={{0,2},{2,4},{4,6},{6,8},{8,10},{10,12},{12,14},{14,0},{1,3},{3,5},... | collective-permute-start | bytes 786440 | tf_op jit(solution)/shard_map/ppermute | solution.py:192
  81.7 11.6 %collective-permute-start.7 = (bf16[32,16,128]{2,1,0:T(8,128)(2,1)S(1)}, bf16[32,16,128]{2,1,0:T(8,128)(2,1)S(1)}, u32[]{:S(2)}, u32[]{:S(2)}) collective-permute-start(bf16[32,16,128]{2,1,0:T(8,128)(2,1)S(1)} %slice.8), channel_id=1, source_target_pairs={{0,2},{2,4},{4,6},{6,8},{8,10},{10,12},{12,14},{14,0},{1,3},{3,5},... | collective-permute-start | bytes 393224 | tf_op jit(solution)/shard_map/ppermute | solution.py:192
  108.8 32.3 %collective-permute-start.9 = (f32[32,104,384]{2,1,0:T(8,128)}, f32[32,104,384]{2,1,0:T(8,128)}, u32[]{:S(2)}, u32[]{:S(2)}) collective-permute-start(f32[32,104,384]{2,1,0:T(8,128)} %get-tuple-element.16), channel_id=1, source_target_pairs={{0,1},{1,0},{2,3},{3,2},{4,5},{5,4},{6,7},{7,6},{8,9},{9,8},{10,11... | collective-permute-start | bytes 15335432 | tf_op jit(solution)/shard_map/ppermute | solution.py:243
  122.7 18.4 %all-to-all-start.3 = ((f32[32,8,128]{2,1,0:T(8,128)}), f32[32,8,128]{2,1,0:T(8,128)S(1)}, u32[]{:S(2)}, u32[]{:S(2)}) async-start(f32[32,8,128]{2,1,0:T(8,128)} %broadcast_in_dim.10), calls=%async_computation.3 | async-start | bytes 262144 | tf_op jit(solution)/shard_map/all_to_all | solution.py:245
  141.1 21.5 %copy-start = (f32[24,3328]{1,0:T(8,128)S(1)}, f32[24,3328]{1,0:T(8,128)}, u32[]{:S(2)}) copy-start(f32[24,3328]{1,0:T(8,128)} %momentum_ref.1) | copy-start | bytes 958468
